TPU v7x, 32 devices: a whole 2x2x4 slice. The times are simulated.
32 devices in a mesh: heads: 2 (over core), tokens: 16 (over z, y, x).
Axes of the slice: x: 2, y: 2, z: 4, core: 2. Of those that a mesh axis runs over, the one named last changes fastest.
Arguments:
- queries: bfloat16 [2, 2048, 2048], P(None, 'tokens', 'heads'), may hold values from -8.5 to 8.5, as said below
- keys: bfloat16 [2, 2048, 2048], P(None, 'tokens', 'heads'), may hold values from -6 to 6
- values: bfloat16 [2, 2048, 2048], P(None, 'tokens', 'heads'), may hold values from -6 to 6
- rates: float32 [2, 8, 2048], P(None, 'heads', 'tokens'), may hold values from 0.05 to 1
- fast_init: bfloat16 [8, 3, 256, 256], P('heads'), may hold values from -0.375 to 0.375
- out_gain: float32 [2048], P('heads'), may hold values from 0.25 to 1.75
Outputs:
- mixed: bfloat16 [2, 2048, 2048], P(None, 'tokens', 'heads')
- final_weights: bfloat16 [8, 3, 256, 256], P('heads')
Inputs may be any that keep to these rules, and one draw needn't show every extreme that they name: queries are real-valued and of order one.
All inputs are finite; a program needn't handle non-finite values.
Results may differ from a plain program's by a relative error of at most 0.0095.
Values may be sent and summed in bfloat16 or wider, within the bound.
A program may use at most 64 MiB of HBM per device.

v0:
```python
import functools

import jax
import jax.numpy as jnp
from jax import lax
from jax.experimental import pallas as pl
from jax.experimental.pallas import tpu as pltpu
from jax.sharding import PartitionSpec as P

D = 2048
NS_STEPS = 2


coef_a = 3.4445
coef_b = -4.775
coef_c = 2.0315
step_size = 0.5


def newton(current):
    for step in range(NS_STEPS):
        gram = jnp.einsum(
            "hmij,hmkj->hmik", current, current, preferred_element_type=jnp.float32
        ).astype(jnp.bfloat16)
        square = jnp.einsum("hmij,hmjk->hmik", gram, gram, preferred_element_type=jnp.float32)
        mixer = (coef_b * gram.astype(jnp.float32) + coef_c * square).astype(jnp.bfloat16)
        product = jnp.einsum("hmij,hmjk->hmik", mixer, current, preferred_element_type=jnp.float32)
        current = (coef_a * current.astype(jnp.float32) + product).astype(jnp.bfloat16)
    return current


def apply_heads(query, weights):
    gate_q = jnp.einsum("nhd,hde->nhe", query, weights[:, 0], preferred_element_type=jnp.float32)
    up_q = jnp.einsum("nhd,hde->nhe", query, weights[:, 1], preferred_element_type=jnp.float32)
    hidden_q = (jax.nn.silu(gate_q) * up_q).astype(jnp.bfloat16)
    return jnp.einsum("nhd,hde->nhe", hidden_q, weights[:, 2], preferred_element_type=jnp.float32)


def local_grads(key_rows, value_rows, rate, weights):
    gate_k = jnp.einsum("nhd,hde->nhe", key_rows, weights[:, 0], preferred_element_type=jnp.float32)
    up_k = jnp.einsum("nhd,hde->nhe", key_rows, weights[:, 1], preferred_element_type=jnp.float32)
    sig = jax.nn.sigmoid(gate_k)
    hidden = (gate_k * sig * up_k).astype(jnp.bfloat16)
    scaled = (rate.T[:, :, None] * value_rows.astype(jnp.float32)).astype(jnp.bfloat16)
    back = jnp.einsum("nhe,hde->nhd", scaled, weights[:, 2], preferred_element_type=jnp.float32)
    grad_gate = (back * up_k * sig * (1.0 + gate_k * (1.0 - sig))).astype(jnp.bfloat16)
    grad_up = (back * gate_k * sig).astype(jnp.bfloat16)
    g_gate = jnp.einsum("nhd,nhe->hde", key_rows, grad_gate, preferred_element_type=jnp.float32)
    g_up = jnp.einsum("nhd,nhe->hde", key_rows, grad_up, preferred_element_type=jnp.float32)
    g_down = jnp.einsum("nhd,nhe->hde", hidden, scaled, preferred_element_type=jnp.float32)
    return jnp.stack([g_gate, g_up, g_down], axis=1)


def finish(joined, totals, out_gain):
    return (joined / jnp.sqrt(totals[:, None] / D + 1e-06) * out_gain[None, :]).astype(jnp.bfloat16)


def per_device(queries, keys, values, rates, fast_init, out_gain):
    heads_here = fast_init.shape[0]
    head_size = fast_init.shape[2]
    tok_rows = queries.shape[1]
    weights = fast_init
    outputs = []
    joined_all = []
    for block in range(queries.shape[0]):
        query = queries[block].reshape(tok_rows, heads_here, head_size)
        key_rows = keys[block].reshape(tok_rows, heads_here, head_size)
        value_rows = values[block].reshape(tok_rows, heads_here, head_size)
        joined = apply_heads(query, weights).reshape(tok_rows, heads_here * head_size)
        grads = local_grads(key_rows, value_rows, rates[block], weights)
        total = lax.psum(grads, "tokens")
        squares = jnp.sum(total * total, axis=(2, 3))
        start = (total / (jnp.sqrt(squares)[:, :, None, None] + 1e-07)).astype(jnp.bfloat16)
        update = newton(start)
        weights = (weights.astype(jnp.float32) + step_size * update.astype(jnp.float32)).astype(
            jnp.bfloat16
        )
        joined_all.append(joined)
    stacked = jnp.stack(joined_all, axis=0)
    totals = lax.psum(jnp.sum(stacked * stacked, axis=2), "heads")
    outputs = [
        finish(joined_all[index], totals[index], out_gain) for index in range(len(joined_all))
    ]
    return (jnp.stack(outputs, axis=0), weights)


F32 = jnp.float32
BF16 = jnp.bfloat16
MESH = pl.DeviceIdType.MESH
DOWN_FIRST = (2, 0, 1)


def mm(a, b):
    return jnp.dot(a, b, preferred_element_type=F32)


def mm_nt(a, b):
    return lax.dot_general(a, b, (((1,), (1,)), ((), ())), preferred_element_type=F32)


def mm_tn(a, b):
    return lax.dot_general(a, b, (((0,), (0,)), ((), ())), preferred_element_type=F32)


def orthogonalize(mats):
    xs = []
    for g in mats:
        g = g.astype(F32)
        square = jnp.sum(jnp.sum(g * g, axis=1, keepdims=True), axis=0, keepdims=True)
        xs.append((g / (jnp.sqrt(square) + 1e-07)).astype(BF16))
    for _ in range(NS_STEPS):
        grams = [mm_nt(x, x).astype(BF16) for x in xs]
        mixers = [(coef_b * a.astype(F32) + coef_c * mm(a, a)).astype(BF16) for a in grams]
        xs = [(coef_a * x.astype(F32) + mm(b, x)).astype(BF16) for b, x in zip(mixers, xs)]
    return xs


def kernel(
    sizes, q_hbm, k_hbm, v_hbm, r_hbm, w_hbm, gain_hbm, mixed, wout,
    q0, w0, rates, gain, kv, q1, hid, dp, dg, du, gf, gb, rs, ag, w1, ysend, ybuf, y0, sq, sqr,
    loc_sem, a2a_s, kv_r, one_r, rs_s, rs_r, ag_s, ag_r, col_s, col_r, fwd_s, fwd_r, y_s, sq_s, sq_r,
):
    cores, HL, G, rows, DH = sizes
    width = HL * DH
    part = DH // G
    half = part // 2
    core = lax.axis_index("heads")
    t = lax.axis_index("tokens")
    z = t // G
    p = t % G
    xn = p + 1 - 2 * (p % 2)
    yn = (p + 2) % G
    across = (xn + 2) % G

    def remote(src, dst, send_sem, recv_sem, device):
        return pltpu.make_async_remote_copy(
            src_ref=src, dst_ref=dst, send_sem=send_sem, recv_sem=recv_sem,
            device_id=device, device_id_type=MESH,
        )

    def send(src, dst, send_sem, recv_sem, device):
        remote(src, dst, send_sem, recv_sem, device).start()

    def head_peer(j):
        return (z + j) % HL

    def head_source(j):
        return (z + HL - j) % HL

    def plane_peer(j):
        return (p + j) % G

    def at(zz, pp):
        return {"tokens": zz * G + pp}

    def arrived(ref, recv_sem):
        remote(ref, ref, loc_sem.at[0], recv_sem, at(z, xn)).wait_recv()

    def drained(ref, send_sem):
        remote(ref, ref, send_sem, loc_sem.at[0], at(z, xn)).wait_send()

    def cols(h):
        return pl.ds(pl.multiple_of(h * DH, DH), DH)

    def part_rows(pp):
        return pl.ds(pl.multiple_of(pp * part, part), part)

    def half_rows(pp, which):
        return pl.ds(pl.multiple_of(pp * part + which * half, half), half)

    local_q = pltpu.make_async_copy(q_hbm.at[0], q0, loc_sem.at[0])
    local_w = pltpu.make_async_copy(w_hbm, w0, loc_sem.at[1])
    local_r = pltpu.make_async_copy(r_hbm, rates.at[z], loc_sem.at[2])
    local_gain = pltpu.make_async_copy(gain_hbm, gain, loc_sem.at[3])
    local_w.start()
    local_q.start()
    local_r.start()
    local_gain.start()
    pieces = [(k_hbm, 0), (v_hbm, 0), (k_hbm, 1), (v_hbm, 1), (q_hbm, 1)]

    def landing(i):
        return q1 if i == 4 else kv.at[i]

    local_pieces = []
    for i, (ref, block) in enumerate(pieces):
        copy = pltpu.make_async_copy(ref.at[block, :, cols(z)], landing(i).at[z], loc_sem.at[4 + i])
        copy.start()
        local_pieces.append(copy)

    barrier = pltpu.get_barrier_semaphore()
    for j in range(1, HL):
        pl.semaphore_signal(barrier, inc=1, device_id=at(head_peer(j), p), device_id_type=MESH)
    for j in range(1, G):
        pl.semaphore_signal(barrier, inc=1, device_id=at(z, plane_peer(j)), device_id_type=MESH)
    for j in range(1, cores):
        pl.semaphore_signal(barrier, inc=1, device_id={"heads": (core + j) % cores}, device_id_type=MESH)
    pl.semaphore_wait(barrier, HL - 1 + G - 1 + cores - 1)

    for j in range(1, HL):
        send(r_hbm, rates.at[z], a2a_s.at[5], one_r.at[0], at(head_peer(j), p))
    for i, (ref, block) in enumerate(pieces):
        for j in range(1, HL):
            h = head_peer(j)
            recv = one_r.at[1] if i == 4 else kv_r.at[block, j - 1]
            send(ref.at[block, :, cols(h)], landing(i).at[z], a2a_s.at[i], recv, at(h, p))

    def share_squares(block, square):
        sq[block] = jnp.broadcast_to(square, (rows, 128))
        for j in range(1, cores):
            send(sq.at[block], sqr.at[block, j - 1], sq_s.at[block], sq_r.at[block],
                 {"heads": (core + j) % cores})

    def finish_block(block, read):
        total = sq[block]
        arrived(sqr.at[block], sq_r.at[block])
        for j in range(1, cores):
            total = total + sqr[block, j - 1]
        root = jnp.sqrt(total[:, :1] / (cores * width) + 1e-06)
        for h in range(HL):
            span = slice(h * DH, (h + 1) * DH)
            mixed[block, :, span] = (read(h) / root * gain[:, span]).astype(BF16)

    def fast_net(x, w_gate, w_up, w_down):
        gate = mm(x, w_gate)
        hidden = (jax.nn.silu(gate) * mm(x, w_up)).astype(BF16)
        return mm(hidden, w_down)

    def share(view, send_sem, recv_x, recv_y, recv_r):
        mine = view(part_rows(p))
        send(mine, mine, send_sem, recv_x, at(z, xn))
        send(mine, mine, send_sem, recv_y, at(z, yn))
        send(mine, mine, send_sem, recv_r, at(z, across))

    def shared(view, recv_x, recv_y):
        arrived(view(part_rows(xn)), recv_x)
        arrived(view(part_rows(yn)), recv_y)

    def pass_on(view, send_sem, recv_x, recv_y, recv_relay):
        arrived(view(part_rows(xn)), recv_x)
        first = view(half_rows(xn, 0))
        send(first, first, send_sem, recv_relay, at(z, yn))
        arrived(view(part_rows(yn)), recv_y)
        second = view(half_rows(yn, 1))
        send(second, second, send_sem, recv_relay, at(z, xn))

    local_w.wait()
    local_q.wait()
    square = jnp.zeros((rows, 1), F32)
    for h in range(HL):
        span = slice(h * DH, (h + 1) * DH)
        y = fast_net(q0[:, span], w0[h, 0], w0[h, 1], w0[h, 2])
        y0[:, span] = y
        square = square + jnp.sum(y * y, axis=1, keepdims=True)
    share_squares(0, square)

    order = [0] + sorted(range(1, HL), key=lambda j: min(j, HL - j))

    def gradients(block, weight):
        for j in order:
            h = head_source(j)
            if j == 0:
                local_pieces[2 * block].wait()
                local_pieces[2 * block + 1].wait()
                if block == 0:
                    local_r.wait()
                    arrived(rates.at[pl.ds(0, HL - 1)], one_r.at[0])
            else:
                arrived(kv.at[pl.ds(2 * block, 2), h], kv_r.at[block, j - 1])
            keys = kv[2 * block, h]
            rate = jnp.broadcast_to(rates[h, block, pl.ds(z, 1), :], (rows, rows)).T[:, :1]
            gate = mm(keys, weight(0))
            up = mm(keys, weight(1))
            sig = jax.nn.sigmoid(gate)
            hid[block, h] = (gate * sig * up).astype(BF16)
            scaled = (rate * kv[2 * block + 1, h].astype(F32)).astype(BF16)
            dp[block, h] = scaled
            back = mm_nt(scaled, weight(2))
            dg[block, h] = (back * up * sig * (1.0 + gate * (1.0 - sig))).astype(BF16)
            du[block, h] = (back * gate * sig).astype(BF16)
        keys = kv[2 * block].reshape(HL * rows, DH)
        pairs = {
            0: lambda: mm_tn(keys, dg[block].reshape(HL * rows, DH)),
            1: lambda: mm_tn(keys, du[block].reshape(HL * rows, DH)),
            2: lambda: mm_tn(hid[block].reshape(HL * rows, DH), dp[block].reshape(HL * rows, DH)),
        }
        for m in DOWN_FIRST:
            grad = pairs[m]()
            gf[block, m] = grad
            gb[block, m] = grad.astype(BF16)
            for j in range(1, G):
                o = plane_peer(j)
                send(gb.at[block, m, part_rows(o)], rs.at[block, m, j - 1], rs_s.at[block],
                     rs_r.at[block, m], at(z, o))

    def ag_view(block, m):
        return lambda span: ag.at[block, m, span]

    def sum_parts(block):
        for m in DOWN_FIRST:
            total = gf[block, m, part_rows(p)]
            arrived(rs.at[block, m], rs_r.at[block, m])
            for j in range(1, G):
                total = total + rs[block, m, j - 1].astype(F32)
            ag[block, m, part_rows(p)] = total.astype(BF16)
            share(ag_view(block, m), ag_s.at[block], ag_r.at[block, m, 0], ag_r.at[block, m, 1], ag_r.at[block, m, 2])
        for m in DOWN_FIRST:
            shared(ag_view(block, m), ag_r.at[block, m, 0], ag_r.at[block, m, 1])

    def summed(block, m):
        arrived(ag.at[block, m, part_rows(across)], ag_r.at[block, m, 2])
        return ag[block, m]

    gradients(0, lambda m: w0[z, m])
    local_gain.wait()
    finish_block(0, lambda h: y0[:, h * DH:(h + 1) * DH])
    sum_parts(0)
    updates = orthogonalize([summed(0, m) for m in DOWN_FIRST])
    for m, x in zip(DOWN_FIRST, updates):
        w1[m] = (w0[z, m].astype(F32) + step_size * x.astype(F32)).astype(BF16)

    gradients(1, lambda m: w1[m])
    local_pieces[4].wait()
    arrived(q1.at[pl.ds(0, HL - 1)], one_r.at[1])
    for j in order:
        h = head_peer(j)
        y = fast_net(q1[h], w1[0], w1[1], w1[2]).astype(BF16)
        if j == 0:
            ybuf[z] = y
        else:
            ysend[h] = y
            send(ysend.at[h], ybuf.at[z], y_s.at[0], one_r.at[2], at(h, p))
    sum_parts(1)
    for m in DOWN_FIRST:
        (x,) = orthogonalize([summed(1, m)])
        wout[z, m] = (w1[m].astype(F32) + step_size * x.astype(F32)).astype(BF16)
        for j in order[1:]:
            mine = wout.at[z, m, part_rows(p)]
            send(mine, mine, col_s.at[0], col_r.at[m, j - 1], at(head_peer(j), p))

    arrived(ybuf.at[pl.ds(0, HL - 1)], one_r.at[2])
    square = jnp.zeros((rows, 1), F32)
    for h in range(HL):
        y = ybuf[h].astype(F32)
        square = square + jnp.sum(y * y, axis=1, keepdims=True)
    share_squares(1, square)

    def wout_view(m, j):
        return lambda span: wout.at[head_source(j), m, span]

    items = [(m, j) for m in DOWN_FIRST for j in order[1:]]
    passed = len(items) - 3
    for n in range(len(items) + 5):
        if n < len(items):
            m, j = items[n]
            recvs = (fwd_r.at[0, m, j - 1], fwd_r.at[1, m, j - 1])
            arrived(wout_view(m, j)(part_rows(p)), col_r.at[m, j - 1])
            if n < passed:
                mine = wout_view(m, j)(part_rows(p))
                send(mine, mine, fwd_s.at[0], recvs[0], at(z, xn))
                send(mine, mine, fwd_s.at[0], recvs[1], at(z, yn))
            else:
                share(wout_view(m, j), fwd_s.at[0], *recvs, one_r.at[3])
        if n >= 5:
            m, j = items[n - 5]
            recvs = (fwd_r.at[0, m, j - 1], fwd_r.at[1, m, j - 1])
            if n - 5 < passed:
                pass_on(wout_view(m, j), fwd_s.at[0], *recvs, one_r.at[3])
            else:
                shared(wout_view(m, j), *recvs)
    finish_block(1, lambda h: ybuf[h].astype(F32))
    arrived(wout.at[pl.ds(0, HL - 1), :, pl.ds(0, part)], one_r.at[3])

    for i in range(5):
        drained(q1.at[pl.ds(0, HL - 1)], a2a_s.at[i])
    drained(rates.at[pl.ds(0, HL - 1)], a2a_s.at[5])
    for block in range(2):
        drained(rs.at[block], rs_s.at[block])
        drained(rs.at[block], ag_s.at[block])
        drained(sqr.at[block], sq_s.at[block])
    drained(wout.at[pl.ds(0, HL - 1), :, pl.ds(0, part)], col_s.at[0])
    drained(wout.at[pl.ds(0, HL - 1), :, pl.ds(0, 3 * part)], fwd_s.at[0])
    drained(ysend.at[pl.ds(0, HL - 1)], y_s.at[0])


def one_kernel(cores, token_devices, queries, keys, values, rates, fast_init, out_gain):
    blocks, rows, width = queries.shape
    HL, _, DH, _ = fast_init.shape
    G = token_devices // HL
    dma = lambda *shape: pltpu.SemaphoreType.DMA(shape)
    tokens = (2, HL, rows, DH)
    mats = (2, 3, DH, DH)
    any_space = pl.BlockSpec(memory_space=pl.ANY)
    in_vmem = pl.BlockSpec(memory_space=pltpu.VMEM)
    return pl.pallas_call(
        functools.partial(kernel, (cores, HL, G, rows, DH)),
        out_shape=(pltpu.VMEM(queries.shape, BF16), pltpu.VMEM(fast_init.shape, BF16)),
        in_specs=[any_space] * 6,
        out_specs=(in_vmem, in_vmem),
        scratch_shapes=[
            pltpu.VMEM((rows, width), BF16),
            pltpu.VMEM(fast_init.shape, BF16),
            pltpu.VMEM((HL,) + rates.shape, F32),
            pltpu.VMEM((1, width), F32),
            pltpu.VMEM((4, HL, rows, DH), BF16),
            pltpu.VMEM((HL, rows, DH), BF16),
            pltpu.VMEM(tokens, BF16),
            pltpu.VMEM(tokens, BF16),
            pltpu.VMEM(tokens, BF16),
            pltpu.VMEM(tokens, BF16),
            pltpu.VMEM(mats, F32),
            pltpu.VMEM(mats, BF16),
            pltpu.VMEM((2, 3, G - 1, DH // G, DH), BF16),
            pltpu.VMEM(mats, BF16),
            pltpu.VMEM((3, DH, DH), BF16),
            pltpu.VMEM((HL, rows, DH), BF16),
            pltpu.VMEM((HL, rows, DH), BF16),
            pltpu.VMEM((rows, width), F32),
            pltpu.VMEM((2, rows, 128), F32),
            pltpu.VMEM((2, cores - 1, rows, 128), F32),
            dma(9),
            dma(6), dma(2, HL - 1), dma(4),
            dma(2), dma(2, 3),
            dma(2), dma(2, 3, 3),
            dma(1), dma(3, HL - 1),
            dma(1), dma(2, 3, HL - 1),
            dma(1), dma(2), dma(2),
        ],
        compiler_params=pltpu.CompilerParams(collective_id=0, has_side_effects=True),
    )(queries, keys, values, rates, fast_init, out_gain.reshape(1, width))


def fits(cores, token_devices, queries, fast_init):
    blocks, rows, width = queries.shape
    HL, _, DH, _ = fast_init.shape
    return (
        blocks == 2 and HL > 1 and cores > 1 and token_devices == 4 * HL
        and rows == 128 and DH % 128 == 0
    )


def per_device_best(cores, token_devices, queries, keys, values, rates, fast_init, out_gain):
    if fits(cores, token_devices, queries, fast_init):
        return one_kernel(cores, token_devices, queries, keys, values, rates, fast_init, out_gain)
    return per_device(queries, keys, values, rates, fast_init, out_gain)


def solution(mesh):
    in_specs = (
        P(None, "tokens", "heads"),
        P(None, "tokens", "heads"),
        P(None, "tokens", "heads"),
        P(None, "heads", "tokens"),
        P("heads", None, None, None),
        P("heads"),
    )
    out_specs = (P(None, "tokens", "heads"), P("heads", None, None, None))
    return jax.shard_map(
        functools.partial(per_device_best, mesh.shape["heads"], mesh.shape["tokens"]), mesh=mesh, in_specs=in_specs, out_specs=out_specs, check_vma=False
    )
```

profile of v0, /device:TPU:0, one launch (start us, length us, event | category | flops | bytes accessed | tf_op | source)
XLA Modules:
  0.0 64.8 jit_solution(14148908173914040641)
XLA Ops:
  0.6 62.2 %shard_map.77 = (bf16[2,128,1024]{2,1,0:T(8,128)(2,1)S(1)}, bf16[4,3,256,256]{3,2,1,0:T(8,128)(2,1)S(1)}) custom-call(bf16[2,128,1024]{2,1,0:T(8,128)(2,1)} %q_hbm.1, bf16[2,128,1024]{2,1,0:T(8,128)(2,1)} %k_hbm.1, bf16[2,128,1024]{2,1,0:T(8,128)(2,1)} %v_hbm.1, f32[2,4,128]{2,1,0:T(4,128)} %r_hbm.1, bf16[4,3,256,256]{3,2,1,0:T(8,128)(2,1)} %w_hbm.1, ...), custom_call_target="tpu_custom_call" | custom-call | tf_op jit(solution)/shard_map/pallas_call | solution.py:394
  62.8 0.8 %copy.10 = bf16[2,128,1024]{2,1,0:T(8,128)(2,1)} copy(bf16[2,128,1024]{2,1,0:T(8,128)(2,1)S(1)} %get-tuple-element.2) | data formatting | bytes 1048576
  63.6 1.1 %copy.11 = bf16[4,3,256,256]{3,2,1,0:T(8,128)(2,1)} copy(bf16[4,3,256,256]{3,2,1,0:T(8,128)(2,1)S(1)} %get-tuple-element.3) | data formatting | bytes 3145728
where the time goes:
time: 64.9 us; the launch traced here: 64.8 us
  Pallas kernels  62.2 us (96%)
  local copies, waits for them, and re-layouts  1.94 us (3%)
    pallas_call x1, Pallas kernels, one_kernel(): pl.pallas_call(functools.partial(kernel, (cores, HL, G, rows, DH)), out_s...  62.2 us
    unnamed x2, local copies, waits for them, and re-layouts  1.94 us

commit v1 on v0

v1 whole, which is shorter than its diff:
```python
import functools

import jax
import jax.numpy as jnp
from jax import lax
from jax.experimental import pallas as pl
from jax.experimental.pallas import tpu as pltpu
from jax.sharding import PartitionSpec as P

D = 2048
NS_STEPS = 2


coef_a = 3.4445
coef_b = -4.775
coef_c = 2.0315
step_size = 0.5


def newton(current):
    for step in range(NS_STEPS):
        gram = jnp.einsum(
            "hmij,hmkj->hmik", current, current, preferred_element_type=jnp.float32
        ).astype(jnp.bfloat16)
        square = jnp.einsum("hmij,hmjk->hmik", gram, gram, preferred_element_type=jnp.float32)
        mixer = (coef_b * gram.astype(jnp.float32) + coef_c * square).astype(jnp.bfloat16)
        product = jnp.einsum("hmij,hmjk->hmik", mixer, current, preferred_element_type=jnp.float32)
        current = (coef_a * current.astype(jnp.float32) + product).astype(jnp.bfloat16)
    return current


def apply_heads(query, weights):
    gate_q = jnp.einsum("nhd,hde->nhe", query, weights[:, 0], preferred_element_type=jnp.float32)
    up_q = jnp.einsum("nhd,hde->nhe", query, weights[:, 1], preferred_element_type=jnp.float32)
    hidden_q = (jax.nn.silu(gate_q) * up_q).astype(jnp.bfloat16)
    return jnp.einsum("nhd,hde->nhe", hidden_q, weights[:, 2], preferred_element_type=jnp.float32)


def local_grads(key_rows, value_rows, rate, weights):
    gate_k = jnp.einsum("nhd,hde->nhe", key_rows, weights[:, 0], preferred_element_type=jnp.float32)
    up_k = jnp.einsum("nhd,hde->nhe", key_rows, weights[:, 1], preferred_element_type=jnp.float32)
    sig = jax.nn.sigmoid(gate_k)
    hidden = (gate_k * sig * up_k).astype(jnp.bfloat16)
    scaled = (rate.T[:, :, None] * value_rows.astype(jnp.float32)).astype(jnp.bfloat16)
    back = jnp.einsum("nhe,hde->nhd", scaled, weights[:, 2], preferred_element_type=jnp.float32)
    grad_gate = (back * up_k * sig * (1.0 + gate_k * (1.0 - sig))).astype(jnp.bfloat16)
    grad_up = (back * gate_k * sig).astype(jnp.bfloat16)
    g_gate = jnp.einsum("nhd,nhe->hde", key_rows, grad_gate, preferred_element_type=jnp.float32)
    g_up = jnp.einsum("nhd,nhe->hde", key_rows, grad_up, preferred_element_type=jnp.float32)
    g_down = jnp.einsum("nhd,nhe->hde", hidden, scaled, preferred_element_type=jnp.float32)
    return jnp.stack([g_gate, g_up, g_down], axis=1)


def finish(joined, totals, out_gain):
    return (joined / jnp.sqrt(totals[:, None] / D + 1e-06) * out_gain[None, :]).astype(jnp.bfloat16)


def per_device(queries, keys, values, rates, fast_init, out_gain):
    heads_here = fast_init.shape[0]
    head_size = fast_init.shape[2]
    tok_rows = queries.shape[1]
    weights = fast_init
    outputs = []
    joined_all = []
    for block in range(queries.shape[0]):
        query = queries[block].reshape(tok_rows, heads_here, head_size)
        key_rows = keys[block].reshape(tok_rows, heads_here, head_size)
        value_rows = values[block].reshape(tok_rows, heads_here, head_size)
        joined = apply_heads(query, weights).reshape(tok_rows, heads_here * head_size)
        grads = local_grads(key_rows, value_rows, rates[block], weights)
        total = lax.psum(grads, "tokens")
        squares = jnp.sum(total * total, axis=(2, 3))
        start = (total / (jnp.sqrt(squares)[:, :, None, None] + 1e-07)).astype(jnp.bfloat16)
        update = newton(start)
        weights = (weights.astype(jnp.float32) + step_size * update.astype(jnp.float32)).astype(
            jnp.bfloat16
        )
        joined_all.append(joined)
    stacked = jnp.stack(joined_all, axis=0)
    totals = lax.psum(jnp.sum(stacked * stacked, axis=2), "heads")
    outputs = [
        finish(joined_all[index], totals[index], out_gain) for index in range(len(joined_all))
    ]
    return (jnp.stack(outputs, axis=0), weights)


F32 = jnp.float32
BF16 = jnp.bfloat16
MESH = pl.DeviceIdType.MESH
DOWN, GATE, UP = 2, 0, 1
ORDER = (DOWN, GATE, UP)


def mm(a, b):
    return jnp.dot(a, b, preferred_element_type=F32)


def mm_nt(a, b):
    return lax.dot_general(a, b, (((1,), (1,)), ((), ())), preferred_element_type=F32)


def mm_tn(a, b):
    return lax.dot_general(a, b, (((0,), (0,)), ((), ())), preferred_element_type=F32)


def orthogonalize(mats):
    xs = []
    for g in mats:
        g = g.astype(F32)
        square = jnp.sum(jnp.sum(g * g, axis=1, keepdims=True), axis=0, keepdims=True)
        xs.append((g / (jnp.sqrt(square) + 1e-07)).astype(BF16))
    for _ in range(NS_STEPS):
        grams = [mm_nt(x, x).astype(BF16) for x in xs]
        mixers = [(coef_b * a.astype(F32) + coef_c * mm(a, a)).astype(BF16) for a in grams]
        xs = [(coef_a * x.astype(F32) + mm(b, x)).astype(BF16) for b, x in zip(mixers, xs)]
    return xs


def kernel(
    sizes, q_hbm, k_hbm, v_hbm, r_hbm, w_hbm, gain_hbm, mixed, wout,
    q0, vals, w0, rates, gain, dps, kv, qb, act, dgu, hid, w_own, w1, wgu, gd_s, gd_r, gg_s, gg_r, full_d, full_g,
    ysend, ybuf, y0, sq, sqr,
    loc_sem, a2a_s, kv_r, q_r, w_sem, fwd_s, x_s, x_r, c_s, c_r, y_sem, sq_s, sq_r, dc_r, ds_r, dist_s,
):
    cores, HL, rows, DH = sizes
    width = HL * DH
    half = DH // 2
    core = lax.axis_index("heads")
    t = lax.axis_index("tokens")
    x, y, zl, zh = t % 2, (t // 2) % 2, (t // 4) % 2, t // 8
    z = t // 4
    kind = (y + zl) % 2
    home = core == kind
    away = core != kind
    away_bit = (core + kind) % 2
    home_bit = 1 - away_bit

    def pick(first, second):
        return jnp.where(kind == 0, first, second)

    def by_core(first, second):
        return jnp.where(core == 0, first, second)

    own_bits = (pick(x, y), pick(y, zl), pick(zl, zh))
    source_slot = by_core(x + 2 * y + 4 * zl, y + 2 * zl + 4 * zh)
    own_head = pick(x + 2 * zl, z)
    mate = pick(t + 8 * (1 - 2 * zh), t + 1 - 2 * x)
    x_near = t + 1 - 2 * x
    y_near = t + 2 * (1 - 2 * y)
    z_near = t + 4 * (1 - 2 * zl)

    def slot(k, flip=0):
        bits = (k % 2, (k // 2) % 2, k // 4 + flip)
        return sum(((own_bits[i] + bits[i]) % 2) * 2 ** i for i in range(3))

    def group_tokens(k, flip=0):
        a, b, c = k % 2, (k // 2) % 2, k // 4 + flip
        first = (x + a) % 2 + 2 * ((y + b) % 2) + 4 * ((zl + c) % 2) + 8 * zh
        second = x + 2 * ((y + a) % 2) + 4 * ((zl + b) % 2) + 8 * ((zh + c) % 2)
        return pick(first, second)

    def owner(j):
        return by_core(j % 2 + 6 * (j // 2) + 8 * zh, x + 2 * (1 - j % 2) + 4 * j)

    def remote(src, dst, send_sem, recv_sem, device):
        return pltpu.make_async_remote_copy(
            src_ref=src, dst_ref=dst, send_sem=send_sem, recv_sem=recv_sem,
            device_id=device, device_id_type=MESH,
        )

    def send(src, dst, send_sem, recv_sem, device):
        remote(src, dst, send_sem, recv_sem, device).start()

    def arrived(ref, recv_sem):
        remote(ref, ref, loc_sem.at[0], recv_sem, {"tokens": x_near}).wait_recv()

    def drained(ref, send_sem):
        remote(ref, ref, send_sem, loc_sem.at[0], {"tokens": x_near}).wait_send()

    def cols(h):
        return pl.ds(pl.multiple_of(h * DH, DH), DH)

    twin = {"heads": 1 - core}

    local_v = [pltpu.make_async_copy(v_hbm.at[b], vals.at[b], loc_sem.at[4 + b]) for b in range(2)]
    local_r = pltpu.make_async_copy(r_hbm, rates, loc_sem.at[2])
    local_q = pltpu.make_async_copy(q_hbm.at[0], q0, loc_sem.at[0])
    local_w = pltpu.make_async_copy(w_hbm, w0, loc_sem.at[1])
    local_gain = pltpu.make_async_copy(gain_hbm, gain, loc_sem.at[3])
    own_w = pltpu.make_async_copy(w_hbm.at[own_head], w_own, w_sem.at[0])
    local_r.start()
    local_v[0].start()
    local_w.start()
    local_q.start()
    local_v[1].start()
    local_gain.start()

    @pl.when(home)
    def _():
        own_w.start()

    barrier = pltpu.get_barrier_semaphore()

    @pl.when(away)
    def _():
        for k in range(8):
            pl.semaphore_signal(
                barrier, inc=1, device_id={"heads": 1 - core, "tokens": group_tokens(k)}, device_id_type=MESH
            )

    for device in ({"tokens": mate}, {"heads": 1 - core}, {"tokens": x_near}, {"tokens": y_near}):
        pl.semaphore_signal(barrier, inc=1, device_id=device, device_id_type=MESH)

    @pl.when(z < 3)
    def _():
        pl.semaphore_signal(barrier, inc=1, device_id={"tokens": t + 4}, device_id_type=MESH)

    @pl.when(z > 0)
    def _():
        pl.semaphore_signal(barrier, inc=1, device_id={"tokens": t - 4}, device_id_type=MESH)

    pl.semaphore_wait(barrier, HL + 4 + 1 + jnp.where((z == 0) | (z == 3), 0, 1))

    base = by_core(x + 2 * zl, z)

    def spread(array, view, landing, recv_sems):
        for k in SPREAD:
            j = (base + k) % HL
            send(view(j), landing.at[source_slot], a2a_s.at[array], recv_sems.at[source_slot],
                 {"heads": 1 - core, "tokens": owner(j)})

    def spread_keys(b):
        spread(2 * b, lambda j: k_hbm.at[b, :, cols(j)], kv.at[2 * b], kv_r.at[2 * b])

    def spread_values(b):
        spread(2 * b + 1, lambda j: dps.at[b, j], kv.at[2 * b + 1], kv_r.at[2 * b + 1])

    def spread_queries():
        spread(4, lambda j: q_hbm.at[1, :, cols(j)], qb, q_r)

    def scale_values(b):
        for j in range(HL):
            rate = jnp.broadcast_to(rates[b, pl.ds(j, 1), :], (rows, rows)).T[:, :1]
            dps[b, j] = (rate * vals[b, :, j * DH:(j + 1) * DH].astype(F32)).astype(BF16)

    spread_keys(0)

    @pl.when(home)
    def _():
        send(w_hbm.at[own_head], w_own, fwd_s.at[5], w_sem.at[0], twin)

    local_r.wait()
    local_v[0].wait()
    scale_values(0)
    spread_values(0)
    local_v[1].wait()
    scale_values(1)
    if EARLY >= 1:
        spread_keys(1)
    if EARLY >= 2:
        spread_values(1)
    if EARLY >= 3:
        spread_queries()

    def share_squares(b, square):
        sq[b] = jnp.broadcast_to(square, (rows, 128))
        send(sq.at[b], sqr.at[b], sq_s.at[b], sq_r.at[b], twin)

    def finish_block(b, read):
        total = sq[b]
        arrived(sqr.at[b], sq_r.at[b])
        total = total + sqr[b]
        root = jnp.sqrt(total[:, :1] / (cores * width) + 1e-06)
        for h in range(HL):
            span = slice(h * DH, (h + 1) * DH)
            mixed[b, :, span] = (read(h) / root * gain[:, span]).astype(BF16)

    def fast_net(rows_in, w_gate, w_up, w_down):
        gate = mm(rows_in, w_gate)
        hidden = (jax.nn.silu(gate) * mm(rows_in, w_up)).astype(BF16)
        return mm(hidden, w_down)

    local_w.wait()
    local_q.wait()
    square = jnp.zeros((rows, 1), F32)
    for h in range(HL):
        span = slice(h * DH, (h + 1) * DH)
        out = fast_net(q0[:, span], w0[h, 0], w0[h, 1], w0[h, 2])
        y0[:, span] = out
        square = square + jnp.sum(out * out, axis=1, keepdims=True)
    share_squares(0, square)

    def halve_weights(w):
        for c in range(2):
            span = slice(c * half, (c + 1) * half)
            wgu[c] = jnp.concatenate([w[GATE, :, span], w[UP, :, span]], axis=1)

    def forward(array, i, when):
        @pl.when(when)
        def _():
            send(kv.at[array, i], kv.at[array, i], fwd_s.at[array], kv_r.at[array, i], twin)

    def gradients(b, w):
        weights = wgu[core]
        w_down = w[DOWN, pl.ds(pl.multiple_of(core * half, half), half), :]
        for k in range(8):
            i = slot(k)
            if b == 0:
                arrived(kv.at[0, i], kv_r.at[0, i])
                forward(0, i, away)
            else:
                @pl.when(home)
                def _():
                    arrived(kv.at[2, i], kv_r.at[2, i])
            act[k] = mm(kv[2 * b, i], weights)
        for k in range(8):
            i = slot(k)
            if b == 0:
                arrived(kv.at[1, i], kv_r.at[1, i])
                forward(1, i, away)
            else:
                @pl.when(home)
                def _():
                    arrived(kv.at[3, i], kv_r.at[3, i])
            back = mm_nt(kv[2 * b + 1, i], w_down)
            gate = act[k, :, :half]
            up = act[k, :, half:]
            sig = jax.nn.sigmoid(gate)
            hid[i] = (gate * sig * up).astype(BF16)
            dgu[i, :, :half] = (back * up * sig * (1.0 + gate * (1.0 - sig))).astype(BF16)
            dgu[i, :, half:] = (back * gate * sig).astype(BF16)
        count = 8 * rows
        grad = mm_tn(hid[...].reshape(count, half), kv[2 * b + 1].reshape(count, DH))
        gd_s[b] = grad.astype(BF16)
        send(gd_s.at[b], gd_r.at[b], x_s.at[b], x_r.at[b, DOWN], {"tokens": mate})
        grad = mm_tn(kv[2 * b].reshape(count, DH), dgu[...].reshape(count, DH)).astype(BF16)
        gg_s[b, GATE] = grad[:, :half]
        send(gg_s.at[b, GATE], gg_r.at[b, GATE], x_s.at[b], x_r.at[b, GATE], {"tokens": mate})
        gg_s[b, UP] = grad[:, half:]
        send(gg_s.at[b, UP], gg_r.at[b, UP], x_s.at[b], x_r.at[b, UP], {"tokens": mate})

    def exchange(b, m):
        if m == DOWN:
            mine, theirs, full = gd_s.at[b], gd_r.at[b], full_d
        else:
            mine, theirs, full = gg_s.at[b, m], gg_r.at[b, m], full_g.at[m]
        arrived(theirs, x_r.at[b, m])
        total = (mine[...].astype(F32) + theirs[...].astype(F32)).astype(BF16)
        full[b, core] = total
        here = full.at[b, core]
        if b == 0:
            send(here, here, c_s.at[b], c_r.at[b, m], twin)
        else:
            @pl.when(away)
            def _():
                send(here, here, c_s.at[b], c_r.at[b, m], twin)

    def whole(b, m):
        full = full_d if m == DOWN else full_g.at[m]
        arrived(full.at[b, 1 - core], c_r.at[b, m])
        if m == DOWN:
            return full_d[b].reshape(DH, DH)
        return jnp.concatenate([full_g[m, b, 0], full_g[m, b, 1]], axis=1)

    @pl.when(home)
    def _():
        own_w.wait()

    @pl.when(away)
    def _():
        arrived(w_own, w_sem.at[0])

    halve_weights(w_own)
    gradients(0, w_own)
    if EARLY < 1:
        spread_keys(1)
    if EARLY < 2:
        spread_values(1)
    local_gain.wait()
    finish_block(0, lambda h: y0[:, h * DH:(h + 1) * DH])
    for m in ORDER:
        exchange(0, m)
    if EARLY < 3:
        spread_queries()

    @pl.when(away)
    def _():
        for array in (2, 3):
            for k in range(8):
                i = slot(k)
                arrived(kv.at[array, i], kv_r.at[array, i])
                send(kv.at[array, i], kv.at[array, i], fwd_s.at[array], kv_r.at[array, i], twin)

    updates = orthogonalize([whole(0, m) for m in ORDER])
    for m, update in zip(ORDER, updates):
        w1[m] = (w_own[m].astype(F32) + step_size * update.astype(F32)).astype(BF16)
    halve_weights(w1)
    gradients(1, w1)

    @pl.when(away)
    def _():
        for k in range(8):
            i = slot(k)
            arrived(qb.at[i], q_r.at[i])
            if k >= 4:
                send(qb.at[i], qb.at[i], fwd_s.at[4], q_r.at[i], twin)

    for k in range(4):
        i = slot(k, home_bit)

        @pl.when(home)
        def _():
            arrived(qb.at[i], q_r.at[i])

        ysend[k] = fast_net(qb[i], w1[GATE], w1[UP], w1[DOWN]).astype(BF16)
        send(ysend.at[k], ybuf.at[own_head], y_sem.at[0], y_sem.at[1],
             {"heads": kind, "tokens": group_tokens(k, home_bit)})

    for m in ORDER:
        exchange(1, m)

    def squares_of_block1():
        arrived(ybuf, y_sem.at[1])
        square = jnp.zeros((rows, 1), F32)
        for h in range(HL):
            out = ybuf[h].astype(F32)
            square = square + jnp.sum(out * out, axis=1, keepdims=True)
        share_squares(1, square)

    def pass_c(m, j, device):
        part = wout.at[j, m]
        send(part, part, dist_s.at[0], dc_r.at[j, m], {"tokens": device})

    def rows_of(j, m, which):
        return wout.at[j, m, pl.ds(pl.multiple_of(which * half, half), half)]

    def pass_s(m, j, which, device):
        part = rows_of(j, m, which)
        send(part, part, dist_s.at[0], ds_r.at[j, m, which], {"tokens": device})

    def along_z(m, j, up, down):
        @pl.when((z < 3) & up)
        def _():
            pass_s(m, j, y, t + 4)

        @pl.when((z > 0) & down)
        def _():
            pass_s(m, j, y, t - 4)

    def start_spread(m):
        @pl.when(core == 0)
        def _():
            pass_c(m, own_head, y_near)
            pass_c(m, own_head, z_near)
            pass_c(m, own_head, x_near)

        @pl.when(core == 1)
        def _():
            pass_s(m, own_head, 1 - y, y_near)
            along_z(m, own_head, True, True)
            pass_s(m, own_head, y, y_near)

    @pl.when(home)
    def _():
        for m in ORDER:
            (update,) = orthogonalize([whole(1, m)])
            wout[own_head, m] = (w1[m].astype(F32) + step_size * update.astype(F32)).astype(BF16)
            start_spread(m)
            if m == ORDER[0]:
                squares_of_block1()

    @pl.when(away)
    def _():
        squares_of_block1()

    @pl.when(core == 0)
    def _():
        near, far = x + 2 * zl, x + 2 * (1 - zl)
        for m in ORDER:
            @pl.when(kind == 1)
            def _():
                arrived(wout.at[near, m], dc_r.at[near, m])
                pass_c(m, near, z_near)
                pass_c(m, near, x_near)

            arrived(wout.at[far, m], dc_r.at[far, m])
            pass_c(m, far, x_near)

    @pl.when(core == 1)
    def _():
        def first(m):
            @pl.when(kind == 0)
            def _():
                arrived(rows_of(z, m, y), ds_r.at[z, m, y])
                along_z(m, z, True, True)

        def later(m, d):
            @pl.when(z >= d)
            def _():
                arrived(rows_of(z - d, m, y), ds_r.at[z - d, m, y])
                along_z(m, z - d, True, False)
                pass_s(m, z - d, y, y_near)

            @pl.when(z + d <= 3)
            def _():
                arrived(rows_of(z + d, m, y), ds_r.at[z + d, m, y])
                along_z(m, z + d, False, True)
                pass_s(m, z + d, y, y_near)

        for step in range(6):
            for i, m in enumerate(ORDER):
                d = step - i
                if d == 0:
                    first(m)
                elif 1 <= d <= 3:
                    later(m, d)

    finish_block(1, lambda h: ybuf[h].astype(F32))

    @pl.when(core == 0)
    def _():
        for m in ORDER:
            for j in (1 - x + 2 * zl, 1 - x + 2 * (1 - zl)):
                arrived(wout.at[j, m], dc_r.at[j, m])
        drained(wout.at[pl.ds(0, 3)], dist_s.at[0])

        @pl.when(kind == 0)
        def _():
            drained(wout.at[0], dist_s.at[0])

    @pl.when(core == 1)
    def _():
        for m in ORDER:
            for d in range(4):
                j = (z + d) % 4
                if d == 0:
                    @pl.when(kind == 0)
                    def _():
                        arrived(rows_of(j, m, 1 - y), ds_r.at[j, m, 1 - y])
                else:
                    arrived(rows_of(j, m, 1 - y), ds_r.at[j, m, 1 - y])
        drained(wout.at[0, :, pl.ds(0, half)], dist_s.at[0])
        drained(wout.at[0], dist_s.at[0])

        @pl.when(kind == 1)
        def _():
            drained(wout.at[0], dist_s.at[0])

        drained(wout.at[0, :, pl.ds(0, half)], dist_s.at[0])

        @pl.when((z == 1) | (z == 2))
        def _():
            drained(wout.at[pl.ds(0, 2)], dist_s.at[0])

    for i in range(5):
        drained(qb.at[pl.ds(0, HL)], a2a_s.at[i])

    @pl.when(away)
    def _():
        for i in range(4):
            drained(qb, fwd_s.at[i])
        drained(qb.at[pl.ds(0, 4)], fwd_s.at[4])
        drained(full_d.at[0], c_s.at[1])
        drained(full_d.at[0, 0], c_s.at[1])

    @pl.when(home)
    def _():
        drained(w_own, fwd_s.at[5])

    for b in range(2):
        drained(full_d.at[0], x_s.at[b])
        drained(full_d.at[0, 0], x_s.at[b])
        drained(sqr.at[b], sq_s.at[b])
    drained(full_d.at[0], c_s.at[0])
    drained(full_d.at[0, 0], c_s.at[0])
    drained(ysend, y_sem.at[0])


SPREAD = (2, 1, 3, 0)
EARLY = 2


def one_kernel(cores, queries, keys, values, rates, fast_init, out_gain):
    blocks, rows, width = queries.shape
    HL, _, DH, _ = fast_init.shape
    half = DH // 2
    dma = lambda *shape: pltpu.SemaphoreType.DMA(shape)
    vm = pltpu.VMEM
    any_space = pl.BlockSpec(memory_space=pl.ANY)
    in_vmem = pl.BlockSpec(memory_space=pltpu.VMEM)
    return pl.pallas_call(
        functools.partial(kernel, (cores, HL, rows, DH)),
        out_shape=(pltpu.VMEM(queries.shape, BF16), pltpu.VMEM(fast_init.shape, BF16)),
        in_specs=[any_space] * 6,
        out_specs=(in_vmem, in_vmem),
        scratch_shapes=[
            vm((rows, width), BF16),
            vm((2, rows, width), BF16),
            vm(fast_init.shape, BF16),
            vm(rates.shape, F32),
            vm((1, width), F32),
            vm((2, HL, rows, DH), BF16),
            vm((4, 8, rows, DH), BF16),
            vm((8, rows, DH), BF16),
            vm((8, rows, DH), F32),
            vm((8, rows, DH), BF16),
            vm((8, rows, half), BF16),
            vm((3, DH, DH), BF16),
            vm((3, DH, DH), BF16),
            vm((2, DH, DH), BF16),
            vm((2, half, DH), BF16),
            vm((2, half, DH), BF16),
            vm((2, 2, DH, half), BF16),
            vm((2, 2, DH, half), BF16),
            vm((2, 2, half, DH), BF16),
            vm((2, 2, 2, DH, half), BF16),
            vm((HL, rows, DH), BF16),
            vm((HL, rows, DH), BF16),
            vm((rows, width), F32),
            vm((2, rows, 128), F32),
            vm((2, rows, 128), F32),
            dma(6),
            dma(5), dma(4, 8), dma(8), dma(1), dma(6),
            dma(2), dma(2, 3), dma(2), dma(2, 3),
            dma(2), dma(2), dma(2),
            dma(4, 3), dma(4, 3, 2), dma(1),
        ],
        compiler_params=pltpu.CompilerParams(collective_id=0, has_side_effects=True),
    )(queries, keys, values, rates, fast_init, out_gain.reshape(1, width))


def fits(cores, token_devices, queries, fast_init):
    blocks, rows, width = queries.shape
    HL, _, DH, _ = fast_init.shape
    return (
        blocks == 2 and HL == 4 and cores == 2 and token_devices == 16
        and rows == 128 and DH == 256
    )


def per_device_best(cores, token_devices, queries, keys, values, rates, fast_init, out_gain):
    if fits(cores, token_devices, queries, fast_init):
        return one_kernel(cores, queries, keys, values, rates, fast_init, out_gain)
    return per_device(queries, keys, values, rates, fast_init, out_gain)


def solution(mesh):
    in_specs = (
        P(None, "tokens", "heads"),
        P(None, "tokens", "heads"),
        P(None, "tokens", "heads"),
        P(None, "heads", "tokens"),
        P("heads", None, None, None),
        P("heads"),
    )
    out_specs = (P(None, "tokens", "heads"), P("heads", None, None, None))
    return jax.shard_map(
        functools.partial(per_device_best, mesh.shape["heads"], mesh.shape["tokens"]), mesh=mesh, in_specs=in_specs, out_specs=out_specs, check_vma=False
    )
```

time: 64.9 us -> 62.1 us (0.957); the launches traced: 64.8 us -> 61.3 us
  Pallas kernels: 62.2 us -> 58.7 us
    pallas_call x1, Pallas kernels: 62.2 us -> 58.7 us  [one_kernel(): pl.pallas_call(functools.partial(kernel, (cores, HL, rows, DH)), out_shap...]
where the time goes in v1:
time: 62.1 us; the launch traced here: 61.3 us
  Pallas kernels  58.7 us (95%)
  local copies, waits for them, and re-layouts  1.94 us (3%)
  between operations  0.64 us (1%)
    pallas_call x1, Pallas kernels, one_kernel(): pl.pallas_call(functools.partial(kernel, (cores, HL, rows, DH)), out_shap...  58.7 us
    unnamed x2, local copies, waits for them, and re-layouts  1.94 us

profile of v1, /device:TPU:0, one launch (start us, length us, event | category | flops | bytes accessed | tf_op | source)
XLA Modules:
  0.0 61.3 jit_solution(7363678212091058476)
XLA Ops:
  0.6 58.7 %shard_map.77 = (bf16[2,128,1024]{2,1,0:T(8,128)(2,1)S(1)}, bf16[4,3,256,256]{3,2,1,0:T(8,128)(2,1)S(1)}) custom-call(bf16[2,128,1024]{2,1,0:T(8,128)(2,1)} %q_hbm.1, bf16[2,128,1024]{2,1,0:T(8,128)(2,1)} %k_hbm.1, bf16[2,128,1024]{2,1,0:T(8,128)(2,1)} %v_hbm.1, f32[2,4,128]{2,1,0:T(4,128)} %r_hbm.1, bf16[4,3,256,256]{3,2,1,0:T(8,128)(2,1)} %w_hbm.1, ...), custom_call_target="tpu_custom_call" | custom-call | tf_op jit(solution)/shard_map/pallas_call | solution.py:591
  59.4 0.8 %copy.10 = bf16[2,128,1024]{2,1,0:T(8,128)(2,1)} copy(bf16[2,128,1024]{2,1,0:T(8,128)(2,1)S(1)} %get-tuple-element.2) | data formatting | bytes 1048576
  60.2 1.1 %copy.11 = bf16[4,3,256,256]{3,2,1,0:T(8,128)(2,1)} copy(bf16[4,3,256,256]{3,2,1,0:T(8,128)(2,1)S(1)} %get-tuple-element.3) | data formatting | bytes 3145728

commit v2 on v1

--- a/solution.py
+++ b/solution.py
@@ -120,7 +120,7 @@
     sizes, q_hbm, k_hbm, v_hbm, r_hbm, w_hbm, gain_hbm, mixed, wout,
     q0, vals, w0, rates, gain, dps, kv, qb, act, dgu, hid, w_own, w1, wgu, gd_s, gd_r, gg_s, gg_r, full_d, full_g,
     ysend, ybuf, y0, sq, sqr,
-    loc_sem, a2a_s, kv_r, q_r, w_sem, fwd_s, x_s, x_r, c_s, c_r, y_sem, sq_s, sq_r, dc_r, ds_r, dist_s,
+    loc_sem, a2a_s, kv_r, q_r, w_sem, fwd_s, x_s, x_r, c_s, c_r, y_sem, sq_s, sq_r, dist_r, dist_s,
 ):
     cores, HL, rows, DH = sizes
     width = HL * DH
@@ -129,38 +129,26 @@
     t = lax.axis_index("tokens")
     x, y, zl, zh = t % 2, (t // 2) % 2, (t // 4) % 2, t // 8
     z = t // 4
-    kind = (y + zl) % 2
+    kind = (x + y + zl) % 2
     home = core == kind
     away = core != kind
-    away_bit = (core + kind) % 2
-    home_bit = 1 - away_bit
-
-    def pick(first, second):
-        return jnp.where(kind == 0, first, second)
-
-    def by_core(first, second):
-        return jnp.where(core == 0, first, second)
-
-    own_bits = (pick(x, y), pick(y, zl), pick(zl, zh))
-    source_slot = by_core(x + 2 * y + 4 * zl, y + 2 * zl + 4 * zh)
-    own_head = pick(x + 2 * zl, z)
-    mate = pick(t + 8 * (1 - 2 * zh), t + 1 - 2 * x)
+
+    own_slot = x + 2 * y + 4 * zl
+    own_head = x + 2 * zl
+    mate = t + 8 * (1 - 2 * zh)
     x_near = t + 1 - 2 * x
     y_near = t + 2 * (1 - 2 * y)
     z_near = t + 4 * (1 - 2 * zl)
 
-    def slot(k, flip=0):
-        bits = (k % 2, (k // 2) % 2, k // 4 + flip)
-        return sum(((own_bits[i] + bits[i]) % 2) * 2 ** i for i in range(3))
-
-    def group_tokens(k, flip=0):
-        a, b, c = k % 2, (k // 2) % 2, k // 4 + flip
-        first = (x + a) % 2 + 2 * ((y + b) % 2) + 4 * ((zl + c) % 2) + 8 * zh
-        second = x + 2 * ((y + a) % 2) + 4 * ((zl + b) % 2) + 8 * ((zh + c) % 2)
-        return pick(first, second)
-
-    def owner(j):
-        return by_core(j % 2 + 6 * (j // 2) + 8 * zh, x + 2 * (1 - j % 2) + 4 * j)
+    def slot(k):
+        return (x + k % 2) % 2 + 2 * ((y + k // 2 % 2) % 2) + 4 * ((zl + k // 4) % 2)
+
+    def head_at(dx, dz):
+        return (x + dx) % 2 + 2 * ((zl + dz) % 2)
+
+    def owner(dx, dz):
+        x0, z0 = (x + dx) % 2, (zl + dz) % 2
+        return x0 + 2 * ((x0 + z0 + core) % 2) + 4 * z0 + 8 * zh
 
     def remote(src, dst, send_sem, recv_sem, device):
         return pltpu.make_async_remote_copy(
@@ -205,29 +193,17 @@
     def _():
         for k in range(8):
             pl.semaphore_signal(
-                barrier, inc=1, device_id={"heads": 1 - core, "tokens": group_tokens(k)}, device_id_type=MESH
+                barrier, inc=1, device_id={"heads": 1 - core, "tokens": slot(k) + 8 * zh}, device_id_type=MESH
             )
 
-    for device in ({"tokens": mate}, {"heads": 1 - core}, {"tokens": x_near}, {"tokens": y_near}):
+    for device in ({"heads": 1 - core}, *({"tokens": chip} for chip in (mate, x_near, y_near, z_near))):
         pl.semaphore_signal(barrier, inc=1, device_id=device, device_id_type=MESH)
-
-    @pl.when(z < 3)
-    def _():
-        pl.semaphore_signal(barrier, inc=1, device_id={"tokens": t + 4}, device_id_type=MESH)
-
-    @pl.when(z > 0)
-    def _():
-        pl.semaphore_signal(barrier, inc=1, device_id={"tokens": t - 4}, device_id_type=MESH)
-
-    pl.semaphore_wait(barrier, HL + 4 + 1 + jnp.where((z == 0) | (z == 3), 0, 1))
-
-    base = by_core(x + 2 * zl, z)
+    pl.semaphore_wait(barrier, HL + 5)
 
     def spread(array, view, landing, recv_sems):
-        for k in SPREAD:
-            j = (base + k) % HL
-            send(view(j), landing.at[source_slot], a2a_s.at[array], recv_sems.at[source_slot],
-                 {"heads": 1 - core, "tokens": owner(j)})
+        for dx, dz in SPREAD:
+            send(view(head_at(dx, dz)), landing.at[own_slot], a2a_s.at[array], recv_sems.at[own_slot],
+                 {"heads": 1 - core, "tokens": owner(dx, dz)})
 
     def spread_keys(b):
         spread(2 * b, lambda j: k_hbm.at[b, :, cols(j)], kv.at[2 * b], kv_r.at[2 * b])
@@ -242,6 +218,11 @@
         for j in range(HL):
             rate = jnp.broadcast_to(rates[b, pl.ds(j, 1), :], (rows, rows)).T[:, :1]
             dps[b, j] = (rate * vals[b, :, j * DH:(j + 1) * DH].astype(F32)).astype(BF16)
+
+    def issue(point):
+        for when, what in zip(ISSUE, (lambda: spread_keys(1), lambda: spread_values(1), spread_queries)):
+            if when == point:
+                what()
 
     spread_keys(0)
 
@@ -255,12 +236,7 @@
     spread_values(0)
     local_v[1].wait()
     scale_values(1)
-    if EARLY >= 1:
-        spread_keys(1)
-    if EARLY >= 2:
-        spread_values(1)
-    if EARLY >= 3:
-        spread_queries()
+    issue(0)
 
     def share_squares(b, square):
         sq[b] = jnp.broadcast_to(square, (rows, 128))
@@ -303,32 +279,38 @@
     def gradients(b, w):
         weights = wgu[core]
         w_down = w[DOWN, pl.ds(pl.multiple_of(core * half, half), half), :]
-        for k in range(8):
-            i = slot(k)
-            if b == 0:
-                arrived(kv.at[0, i], kv_r.at[0, i])
-                forward(0, i, away)
-            else:
-                @pl.when(home)
-                def _():
-                    arrived(kv.at[2, i], kv_r.at[2, i])
-            act[k] = mm(kv[2 * b, i], weights)
-        for k in range(8):
-            i = slot(k)
-            if b == 0:
-                arrived(kv.at[1, i], kv_r.at[1, i])
-                forward(1, i, away)
-            else:
-                @pl.when(home)
-                def _():
-                    arrived(kv.at[3, i], kv_r.at[3, i])
-            back = mm_nt(kv[2 * b + 1, i], w_down)
-            gate = act[k, :, :half]
-            up = act[k, :, half:]
+        def activations(i, gate_up, back):
+            gate = gate_up[:, :half]
+            up = gate_up[:, half:]
             sig = jax.nn.sigmoid(gate)
             hid[i] = (gate * sig * up).astype(BF16)
             dgu[i, :, :half] = (back * up * sig * (1.0 + gate * (1.0 - sig))).astype(BF16)
             dgu[i, :, half:] = (back * gate * sig).astype(BF16)
+
+        if b == 0:
+            for k in range(8):
+                i = slot(k)
+                arrived(kv.at[0, i], kv_r.at[0, i])
+                forward(0, i, away)
+                act[k] = mm(kv[0, i], weights)
+            for k in range(8):
+                i = slot(k)
+                arrived(kv.at[1, i], kv_r.at[1, i])
+                forward(1, i, away)
+                activations(i, act[k], mm_nt(kv[1, i], w_down))
+                if k == 3:
+                    issue(1)
+            issue(2)
+        else:
+            @pl.when(home)
+            def _():
+                for k in range(8):
+                    i = slot(k)
+                    arrived(kv.at[2, i], kv_r.at[2, i])
+                    arrived(kv.at[3, i], kv_r.at[3, i])
+
+            for i in range(8):
+                activations(i, mm(kv[2, i], weights), mm_nt(kv[3, i], w_down))
         count = 8 * rows
         grad = mm_tn(hid[...].reshape(count, half), kv[2 * b + 1].reshape(count, DH))
         gd_s[b] = grad.astype(BF16)
@@ -372,26 +354,30 @@
 
     halve_weights(w_own)
     gradients(0, w_own)
-    if EARLY < 1:
-        spread_keys(1)
-    if EARLY < 2:
-        spread_values(1)
+    issue(3)
     local_gain.wait()
     finish_block(0, lambda h: y0[:, h * DH:(h + 1) * DH])
     for m in ORDER:
         exchange(0, m)
-    if EARLY < 3:
-        spread_queries()
-
-    @pl.when(away)
-    def _():
-        for array in (2, 3):
+    issue(4)
+
+    def pass_on(array):
+        @pl.when(away)
+        def _():
             for k in range(8):
                 i = slot(k)
                 arrived(kv.at[array, i], kv_r.at[array, i])
                 send(kv.at[array, i], kv.at[array, i], fwd_s.at[array], kv_r.at[array, i], twin)
 
+    if PASS_EARLY >= 1:
+        pass_on(2)
+    if PASS_EARLY >= 2:
+        pass_on(3)
     updates = orthogonalize([whole(0, m) for m in ORDER])
+    if PASS_EARLY < 1:
+        pass_on(2)
+    if PASS_EARLY < 2:
+        pass_on(3)
     for m, update in zip(ORDER, updates):
         w1[m] = (w_own[m].astype(F32) + step_size * update.astype(F32)).astype(BF16)
     halve_weights(w1)
@@ -399,22 +385,11 @@
 
     @pl.when(away)
     def _():
-        for k in range(8):
-            i = slot(k)
+        for i in range(8):
             arrived(qb.at[i], q_r.at[i])
-            if k >= 4:
-                send(qb.at[i], qb.at[i], fwd_s.at[4], q_r.at[i], twin)
-
-    for k in range(4):
-        i = slot(k, home_bit)
-
-        @pl.when(home)
-        def _():
-            arrived(qb.at[i], q_r.at[i])
-
-        ysend[k] = fast_net(qb[i], w1[GATE], w1[UP], w1[DOWN]).astype(BF16)
-        send(ysend.at[k], ybuf.at[own_head], y_sem.at[0], y_sem.at[1],
-             {"heads": kind, "tokens": group_tokens(k, home_bit)})
+        for i in range(8):
+            ysend[i] = fast_net(qb[i], w1[GATE], w1[UP], w1[DOWN]).astype(BF16)
+            send(ysend.at[i], ybuf.at[own_head], y_sem.at[0], y_sem.at[1], {"heads": kind, "tokens": i + 8 * zh})
 
     for m in ORDER:
         exchange(1, m)
@@ -427,38 +402,20 @@
             square = square + jnp.sum(out * out, axis=1, keepdims=True)
         share_squares(1, square)
 
-    def pass_c(m, j, device):
-        part = wout.at[j, m]
-        send(part, part, dist_s.at[0], dc_r.at[j, m], {"tokens": device})
-
     def rows_of(j, m, which):
-        return wout.at[j, m, pl.ds(pl.multiple_of(which * half, half), half)]
-
-    def pass_s(m, j, which, device):
+        return wout.at[j, m, pl.ds(which * half, half)]
+
+    def wait_part(j, m, which):
+        arrived(rows_of(j, m, which), dist_r.at[j, m, which])
+
+    def pass_part(j, m, which, device):
         part = rows_of(j, m, which)
-        send(part, part, dist_s.at[0], ds_r.at[j, m, which], {"tokens": device})
-
-    def along_z(m, j, up, down):
-        @pl.when((z < 3) & up)
-        def _():
-            pass_s(m, j, y, t + 4)
-
-        @pl.when((z > 0) & down)
-        def _():
-            pass_s(m, j, y, t - 4)
+        send(part, part, dist_s.at[0], dist_r.at[j, m, which], {"tokens": device})
 
     def start_spread(m):
-        @pl.when(core == 0)
-        def _():
-            pass_c(m, own_head, y_near)
-            pass_c(m, own_head, z_near)
-            pass_c(m, own_head, x_near)
-
-        @pl.when(core == 1)
-        def _():
-            pass_s(m, own_head, 1 - y, y_near)
-            along_z(m, own_head, True, True)
-            pass_s(m, own_head, y, y_near)
+        for which in range(2):
+            for chip in (x_near, y_near, z_near):
+                pass_part(own_head, m, which, chip)
 
     @pl.when(home)
     def _():
@@ -466,91 +423,52 @@
             (update,) = orthogonalize([whole(1, m)])
             wout[own_head, m] = (w1[m].astype(F32) + step_size * update.astype(F32)).astype(BF16)
             start_spread(m)
-            if m == ORDER[0]:
+
+    by_x, by_y, by_z = head_at(1, 0), head_at(0, 0), head_at(0, 1)
+    opposite = head_at(1, 1)
+
+    @pl.when(away)
+    def _():
+        for m in ORDER:
+            if m == ORDER[2]:
                 squares_of_block1()
+            for which in range(2):
+                for j, chip in ((by_x, z_near), (by_y, x_near), (by_z, y_near)):
+                    wait_part(j, m, which)
+                    pass_part(j, m, which, chip)
+
+    relays = ((by_z, x_near), (opposite, y_near), (by_x, z_near))
+
+    @pl.when(home)
+    def _():
+        for n, (m, (j, chip)) in enumerate(zip(ORDER, relays)):
+            if n == 2:
+                squares_of_block1()
+            for which in range(2):
+                wait_part(j, m, which)
+                pass_part(j, m, which, chip)
+
+    finish_block(1, lambda h: ybuf[h].astype(F32))
 
     @pl.when(away)
     def _():
-        squares_of_block1()
-
-    @pl.when(core == 0)
-    def _():
-        near, far = x + 2 * zl, x + 2 * (1 - zl)
         for m in ORDER:
-            @pl.when(kind == 1)
-            def _():
-                arrived(wout.at[near, m], dc_r.at[near, m])
-                pass_c(m, near, z_near)
-                pass_c(m, near, x_near)
-
-            arrived(wout.at[far, m], dc_r.at[far, m])
-            pass_c(m, far, x_near)
-
-    @pl.when(core == 1)
-    def _():
-        def first(m):
-            @pl.when(kind == 0)
-            def _():
-                arrived(rows_of(z, m, y), ds_r.at[z, m, y])
-                along_z(m, z, True, True)
-
-        def later(m, d):
-            @pl.when(z >= d)
-            def _():
-                arrived(rows_of(z - d, m, y), ds_r.at[z - d, m, y])
-                along_z(m, z - d, True, False)
-                pass_s(m, z - d, y, y_near)
-
-            @pl.when(z + d <= 3)
-            def _():
-                arrived(rows_of(z + d, m, y), ds_r.at[z + d, m, y])
-                along_z(m, z + d, False, True)
-                pass_s(m, z + d, y, y_near)
-
-        for step in range(6):
-            for i, m in enumerate(ORDER):
-                d = step - i
-                if d == 0:
-                    first(m)
-                elif 1 <= d <= 3:
-                    later(m, d)
-
-    finish_block(1, lambda h: ybuf[h].astype(F32))
-
-    @pl.when(core == 0)
-    def _():
-        for m in ORDER:
-            for j in (1 - x + 2 * zl, 1 - x + 2 * (1 - zl)):
-                arrived(wout.at[j, m], dc_r.at[j, m])
-        drained(wout.at[pl.ds(0, 3)], dist_s.at[0])
-
-        @pl.when(kind == 0)
-        def _():
-            drained(wout.at[0], dist_s.at[0])
-
-    @pl.when(core == 1)
-    def _():
-        for m in ORDER:
-            for d in range(4):
-                j = (z + d) % 4
-                if d == 0:
-                    @pl.when(kind == 0)
-                    def _():
-                        arrived(rows_of(j, m, 1 - y), ds_r.at[j, m, 1 - y])
-                else:
-                    arrived(rows_of(j, m, 1 - y), ds_r.at[j, m, 1 - y])
-        drained(wout.at[0, :, pl.ds(0, half)], dist_s.at[0])
+            for which in range(2):
+                wait_part(opposite, m, which)
+
+    @pl.when(home)
+    def _():
+        for m, (relayed, _) in zip(ORDER, relays):
+            for j, _ in relays:
+                if j is not relayed:
+                    for which in range(2):
+                        wait_part(j, m, which)
+
+    drained(wout.at[pl.ds(0, 3)], dist_s.at[0])
+
+    @pl.when(home)
+    def _():
         drained(wout.at[0], dist_s.at[0])
-
-        @pl.when(kind == 1)
-        def _():
-            drained(wout.at[0], dist_s.at[0])
-
-        drained(wout.at[0, :, pl.ds(0, half)], dist_s.at[0])
-
-        @pl.when((z == 1) | (z == 2))
-        def _():
-            drained(wout.at[pl.ds(0, 2)], dist_s.at[0])
 
     for i in range(5):
         drained(qb.at[pl.ds(0, HL)], a2a_s.at[i])
@@ -559,7 +477,7 @@
     def _():
         for i in range(4):
             drained(qb, fwd_s.at[i])
-        drained(qb.at[pl.ds(0, 4)], fwd_s.at[4])
+        drained(ysend, y_sem.at[0])
         drained(full_d.at[0], c_s.at[1])
         drained(full_d.at[0, 0], c_s.at[1])
 
@@ -573,11 +491,11 @@
         drained(sqr.at[b], sq_s.at[b])
     drained(full_d.at[0], c_s.at[0])
     drained(full_d.at[0, 0], c_s.at[0])
-    drained(ysend, y_sem.at[0])
-
-
-SPREAD = (2, 1, 3, 0)
-EARLY = 2
+
+
+SPREAD = ((1, 1), (1, 0), (0, 1), (0, 0))
+ISSUE = (0, 1, 4)
+PASS_EARLY = 2
 
 
 def one_kernel(cores, queries, keys, values, rates, fast_init, out_gain):
@@ -614,7 +532,7 @@
             vm((2, 2, DH, half), BF16),
             vm((2, 2, half, DH), BF16),
             vm((2, 2, 2, DH, half), BF16),
-            vm((HL, rows, DH), BF16),
+            vm((8, rows, DH), BF16),
             vm((HL, rows, DH), BF16),
             vm((rows, width), F32),
             vm((2, rows, 128), F32),
@@ -623,7 +541,7 @@
             dma(5), dma(4, 8), dma(8), dma(1), dma(6),
             dma(2), dma(2, 3), dma(2), dma(2, 3),
             dma(2), dma(2), dma(2),
-            dma(4, 3), dma(4, 3, 2), dma(1),
+            dma(4, 3, 2), dma(1),
         ],
         compiler_params=pltpu.CompilerParams(collective_id=0, has_side_effects=True),
     )(queries, keys, values, rates, fast_init, out_gain.reshape(1, width))

time: 62.1 us -> 55.8 us (0.90); the launches traced: 61.3 us -> 55.7 us
  Pallas kernels: 58.7 us -> 53.1 us
    pallas_call x1, Pallas kernels: 58.7 us -> 53.1 us  [one_kernel(): pl.pallas_call(functools.partial(kernel, (cores, HL, rows, DH)), out_shap...]
where the time goes in v2:
time: 55.8 us; the launch traced here: 55.7 us
  Pallas kernels  53.1 us (95%)
  local copies, waits for them, and re-layouts  1.94 us (3%)
  between operations  0.64 us (1%)
    pallas_call x1, Pallas kernels, one_kernel(): pl.pallas_call(functools.partial(kernel, (cores, HL, rows, DH)), out_shap...  53.1 us
    unnamed x2, local copies, waits for them, and re-layouts  1.94 us

profile of v2, /device:TPU:0, one launch (start us, length us, event | category | flops | bytes accessed | tf_op | source)
XLA Modules:
  0.0 55.7 jit_solution(1692176731380175545)
XLA Ops:
  0.6 53.1 %shard_map.77 = (bf16[2,128,1024]{2,1,0:T(8,128)(2,1)S(1)}, bf16[4,3,256,256]{3,2,1,0:T(8,128)(2,1)S(1)}) custom-call(bf16[2,128,1024]{2,1,0:T(8,128)(2,1)} %q_hbm.1, bf16[2,128,1024]{2,1,0:T(8,128)(2,1)} %k_hbm.1, bf16[2,128,1024]{2,1,0:T(8,128)(2,1)} %v_hbm.1, f32[2,4,128]{2,1,0:T(4,128)} %r_hbm.1, bf16[4,3,256,256]{3,2,1,0:T(8,128)(2,1)} %w_hbm.1, ...), custom_call_target="tpu_custom_call" | custom-call | tf_op jit(solution)/shard_map/pallas_call | solution.py:509
  53.8 0.8 %copy.10 = bf16[2,128,1024]{2,1,0:T(8,128)(2,1)} copy(bf16[2,128,1024]{2,1,0:T(8,128)(2,1)S(1)} %get-tuple-element.2) | data formatting | bytes 1048576
  54.6 1.1 %copy.11 = bf16[4,3,256,256]{3,2,1,0:T(8,128)(2,1)} copy(bf16[4,3,256,256]{3,2,1,0:T(8,128)(2,1)S(1)} %get-tuple-element.3) | data formatting | bytes 3145728

commit v3 on v2

--- a/solution.py
+++ b/solution.py
@@ -118,7 +118,7 @@
 
 def kernel(
     sizes, q_hbm, k_hbm, v_hbm, r_hbm, w_hbm, gain_hbm, mixed, wout,
-    q0, vals, w0, rates, gain, dps, kv, qb, act, dgu, hid, w_own, w1, wgu, gd_s, gd_r, gg_s, gg_r, full_d, full_g,
+    q0, keys0, vals, w0, rates, gain, dps, kv, qb, act, dgu, hid, w_own, w1, wgu, gd_s, gd_r, gg_s, gg_r, full_d, full_g,
     ysend, ybuf, y0, sq, sqr,
     loc_sem, a2a_s, kv_r, q_r, w_sem, fwd_s, x_s, x_r, c_s, c_r, y_sem, sq_s, sq_r, dist_r, dist_s,
 ):
@@ -176,6 +176,8 @@
     local_w = pltpu.make_async_copy(w_hbm, w0, loc_sem.at[1])
     local_gain = pltpu.make_async_copy(gain_hbm, gain, loc_sem.at[3])
     own_w = pltpu.make_async_copy(w_hbm.at[own_head], w_own, w_sem.at[0])
+    local_k = pltpu.make_async_copy(k_hbm.at[0], keys0, loc_sem.at[6])
+    local_k.start()
     local_r.start()
     local_v[0].start()
     local_w.start()
@@ -200,19 +202,19 @@
         pl.semaphore_signal(barrier, inc=1, device_id=device, device_id_type=MESH)
     pl.semaphore_wait(barrier, HL + 5)
 
-    def spread(array, view, landing, recv_sems):
+    def spread(array, view, landing, recv_sems, both=False):
         for dx, dz in SPREAD:
             send(view(head_at(dx, dz)), landing.at[own_slot], a2a_s.at[array], recv_sems.at[own_slot],
-                 {"heads": 1 - core, "tokens": owner(dx, dz)})
+                 {"heads": core if both and dz else 1 - core, "tokens": owner(dx, dz)})
 
     def spread_keys(b):
-        spread(2 * b, lambda j: k_hbm.at[b, :, cols(j)], kv.at[2 * b], kv_r.at[2 * b])
+        spread(2 * b, lambda j: (k_hbm.at[b, :, cols(j)] if b else keys0.at[:, cols(j)]), kv.at[2 * b], kv_r.at[2 * b])
 
     def spread_values(b):
         spread(2 * b + 1, lambda j: dps.at[b, j], kv.at[2 * b + 1], kv_r.at[2 * b + 1])
 
     def spread_queries():
-        spread(4, lambda j: q_hbm.at[1, :, cols(j)], qb, q_r)
+        spread(4, lambda j: q_hbm.at[1, :, cols(j)], qb, q_r, both=True)
 
     def scale_values(b):
         for j in range(HL):
@@ -224,6 +226,7 @@
             if when == point:
                 what()
 
+    local_k.wait()
     spread_keys(0)
 
     @pl.when(home)
@@ -288,17 +291,17 @@
             dgu[i, :, half:] = (back * gate * sig).astype(BF16)
 
         if b == 0:
-            for k in range(8):
+            for k in WAITS:
                 i = slot(k)
                 arrived(kv.at[0, i], kv_r.at[0, i])
                 forward(0, i, away)
                 act[k] = mm(kv[0, i], weights)
-            for k in range(8):
+            for n, k in enumerate(WAITS):
                 i = slot(k)
                 arrived(kv.at[1, i], kv_r.at[1, i])
                 forward(1, i, away)
                 activations(i, act[k], mm_nt(kv[1, i], w_down))
-                if k == 3:
+                if n == 3:
                     issue(1)
             issue(2)
         else:
@@ -383,16 +386,16 @@
     halve_weights(w1)
     gradients(1, w1)
 
-    @pl.when(away)
-    def _():
-        for i in range(8):
-            arrived(qb.at[i], q_r.at[i])
-        for i in range(8):
-            ysend[i] = fast_net(qb[i], w1[GATE], w1[UP], w1[DOWN]).astype(BF16)
-            send(ysend.at[i], ybuf.at[own_head], y_sem.at[0], y_sem.at[1], {"heads": kind, "tokens": i + 8 * zh})
-
-    for m in ORDER:
-        exchange(1, m)
+    def slot_of(k):
+        return (own_slot + 4 * home.astype(jnp.int32)) // 4 % 2 * 4 + k
+
+    def new_outputs(first, last):
+        for k in range(first, last):
+            arrived(qb.at[slot_of(k)], q_r.at[slot_of(k)])
+        for k in range(first, last):
+            i = slot_of(k)
+            ysend[k] = fast_net(qb[i], w1[GATE], w1[UP], w1[DOWN]).astype(BF16)
+            send(ysend.at[k], ybuf.at[own_head], y_sem.at[0], y_sem.at[1], {"heads": kind, "tokens": i + 8 * zh})
 
     def squares_of_block1():
         arrived(ybuf, y_sem.at[1])
@@ -417,25 +420,40 @@
             for chip in (x_near, y_near, z_near):
                 pass_part(own_head, m, which, chip)
 
-    @pl.when(home)
-    def _():
-        for m in ORDER:
+    def last_step(m):
+        @pl.when(home)
+        def _():
             (update,) = orthogonalize([whole(1, m)])
             wout[own_head, m] = (w1[m].astype(F32) + step_size * update.astype(F32)).astype(BF16)
             start_spread(m)
 
+    for n, m in enumerate(ORDER):
+        new_outputs(CUTS[n], CUTS[n + 1])
+        exchange(1, m)
+        last_step(m)
+    new_outputs(CUTS[3], 4)
+
     by_x, by_y, by_z = head_at(1, 0), head_at(0, 0), head_at(0, 1)
     opposite = head_at(1, 1)
 
+    def relay(j, m, chip):
+        for which in range(2):
+            wait_part(j, m, which)
+            pass_part(j, m, which, chip)
+
     @pl.when(away)
     def _():
-        for m in ORDER:
-            if m == ORDER[2]:
-                squares_of_block1()
-            for which in range(2):
-                for j, chip in ((by_x, z_near), (by_y, x_near), (by_z, y_near)):
-                    wait_part(j, m, which)
-                    pass_part(j, m, which, chip)
+        first, second, third = ORDER
+        relay(by_z, first, y_near)
+        relay(by_x, second, z_near)
+        relay(by_x, first, z_near)
+        relay(by_y, first, x_near)
+        squares_of_block1()
+        relay(by_y, third, x_near)
+        relay(by_y, second, x_near)
+        relay(by_z, second, y_near)
+        relay(by_x, third, z_near)
+        relay(by_z, third, y_near)
 
     relays = ((by_z, x_near), (opposite, y_near), (by_x, z_near))
 
@@ -444,9 +462,7 @@
         for n, (m, (j, chip)) in enumerate(zip(ORDER, relays)):
             if n == 2:
                 squares_of_block1()
-            for which in range(2):
-                wait_part(j, m, which)
-                pass_part(j, m, which, chip)
+            relay(j, m, chip)
 
     finish_block(1, lambda h: ybuf[h].astype(F32))
 
@@ -477,7 +493,6 @@
     def _():
         for i in range(4):
             drained(qb, fwd_s.at[i])
-        drained(ysend, y_sem.at[0])
         drained(full_d.at[0], c_s.at[1])
         drained(full_d.at[0, 0], c_s.at[1])
 
@@ -491,11 +506,14 @@
         drained(sqr.at[b], sq_s.at[b])
     drained(full_d.at[0], c_s.at[0])
     drained(full_d.at[0, 0], c_s.at[0])
-
-
+    drained(ysend, y_sem.at[0])
+
+
+WAITS = (0, 7, 3, 5, 6, 1, 2, 4)
 SPREAD = ((1, 1), (1, 0), (0, 1), (0, 0))
 ISSUE = (0, 1, 4)
 PASS_EARLY = 2
+CUTS = (0, 4, 4, 4)
 
 
 def one_kernel(cores, queries, keys, values, rates, fast_init, out_gain):
@@ -506,12 +524,13 @@
     vm = pltpu.VMEM
     any_space = pl.BlockSpec(memory_space=pl.ANY)
     in_vmem = pl.BlockSpec(memory_space=pltpu.VMEM)
-    return pl.pallas_call(
+    results = pl.pallas_call(
         functools.partial(kernel, (cores, HL, rows, DH)),
         out_shape=(pltpu.VMEM(queries.shape, BF16), pltpu.VMEM(fast_init.shape, BF16)),
         in_specs=[any_space] * 6,
         out_specs=(in_vmem, in_vmem),
         scratch_shapes=[
+            vm((rows, width), BF16),
             vm((rows, width), BF16),
             vm((2, rows, width), BF16),
             vm(fast_init.shape, BF16),
@@ -532,12 +551,12 @@
             vm((2, 2, DH, half), BF16),
             vm((2, 2, half, DH), BF16),
             vm((2, 2, 2, DH, half), BF16),
-            vm((8, rows, DH), BF16),
+            vm((HL, rows, DH), BF16),
             vm((HL, rows, DH), BF16),
             vm((rows, width), F32),
             vm((2, rows, 128), F32),
             vm((2, rows, 128), F32),
-            dma(6),
+            dma(7),
             dma(5), dma(4, 8), dma(8), dma(1), dma(6),
             dma(2), dma(2, 3), dma(2), dma(2, 3),
             dma(2), dma(2), dma(2),
@@ -545,6 +564,26 @@
         ],
         compiler_params=pltpu.CompilerParams(collective_id=0, has_side_effects=True),
     )(queries, keys, values, rates, fast_init, out_gain.reshape(1, width))
+    return store(*results)
+
+
+def store_kernel(mixed, weights, mixed_out, weights_out, sems):
+    copies = [pltpu.make_async_copy(mixed.at[b], mixed_out.at[b], sems.at[b]) for b in range(2)]
+    copies += [pltpu.make_async_copy(weights.at[h], weights_out.at[h], sems.at[2 + h]) for h in range(weights.shape[0])]
+    for copy in copies:
+        copy.start()
+    for copy in copies:
+        copy.wait()
+
+
+def store(mixed, weights):
+    return pl.pallas_call(
+        store_kernel,
+        out_shape=(jax.ShapeDtypeStruct(mixed.shape, BF16), jax.ShapeDtypeStruct(weights.shape, BF16)),
+        in_specs=[pl.BlockSpec(memory_space=pl.ANY)] * 2,
+        out_specs=(pl.BlockSpec(memory_space=pltpu.HBM), pl.BlockSpec(memory_space=pltpu.HBM)),
+        scratch_shapes=[pltpu.SemaphoreType.DMA((2 + weights.shape[0],))],
+    )(*(pltpu.with_memory_space_constraint(a, pltpu.VMEM) for a in (mixed, weights)))
 
 
 def fits(cores, token_devices, queries, fast_init):

time: 55.8 us -> 53.1 us (0.952)
  local copies, waits for them, and re-layouts: 1.94 us -> 0 us
  Pallas kernels: 53.1 us -> 52.3 us
    pallas_call x1, Pallas kernels: 53.1 us -> 51 us  [one_kernel(): pl.pallas_call(functools.partial(kernel, (cores, HL, rows, DH)), out_shap...]
    unnamed x2 -> x0, local copies, waits for them, and re-layouts: 1.94 us -> none
    pallas_call x0 -> x1, Pallas kernels: none -> 1.36 us  [store(): pl.pallas_call(store_kernel, out_shape=(jax.ShapeDtypeStruct(mixed.shape,...]
where the time goes in v3:
time: 53.1 us; the launch traced here: 53 us
  Pallas kernels  52.3 us (98%)
  between operations  0.64 us (1%)
    pallas_call x1, Pallas kernels, one_kernel(): pl.pallas_call(functools.partial(kernel, (cores, HL, rows, DH)), out_shap...  51 us
    pallas_call x1, Pallas kernels, store(): pl.pallas_call(store_kernel, out_shape=(jax.ShapeDtypeStruct(mixed.shape,...  1.36 us

profile of v3, /device:TPU:0, one launch (start us, length us, event | category | flops | bytes accessed | tf_op | source)
XLA Modules:
  0.0 53.0 jit_solution(13873931842768133742)
XLA Ops:
  0.6 51.0 %shard_map.77 = (bf16[2,128,1024]{2,1,0:T(8,128)(2,1)S(1)}, bf16[4,3,256,256]{3,2,1,0:T(8,128)(2,1)S(1)}) custom-call(bf16[2,128,1024]{2,1,0:T(8,128)(2,1)} %q_hbm.1, bf16[2,128,1024]{2,1,0:T(8,128)(2,1)} %k_hbm.1, bf16[2,128,1024]{2,1,0:T(8,128)(2,1)} %v_hbm.1, f32[2,4,128]{2,1,0:T(4,128)} %r_hbm.1, bf16[4,3,256,256]{3,2,1,0:T(8,128)(2,1)} %w_hbm.1, ...), custom_call_target="tpu_custom_call" | custom-call | tf_op jit(solution)/shard_map/pallas_call | solution.py:527
  51.6 1.4 %shard_map.78 = (bf16[2,128,1024]{2,1,0:T(8,128)(2,1)}, bf16[4,3,256,256]{3,2,1,0:T(8,128)(2,1)}) custom-call(bf16[2,128,1024]{2,1,0:T(8,128)(2,1)S(1)} %get-tuple-element.4.mixed, bf16[4,3,256,256]{3,2,1,0:T(8,128)(2,1)S(1)} %get-tuple-element.5.weights), custom_call_target="tpu_custom_call" | custom-call | tf_op jit(solution)/shard_map/pallas_call | solution.py:580

commit v4 on v3

--- a/solution.py
+++ b/solution.py
@@ -120,7 +120,7 @@
     sizes, q_hbm, k_hbm, v_hbm, r_hbm, w_hbm, gain_hbm, mixed, wout,
     q0, keys0, vals, w0, rates, gain, dps, kv, qb, act, dgu, hid, w_own, w1, wgu, gd_s, gd_r, gg_s, gg_r, full_d, full_g,
     ysend, ybuf, y0, sq, sqr,
-    loc_sem, a2a_s, kv_r, q_r, w_sem, fwd_s, x_s, x_r, c_s, c_r, y_sem, sq_s, sq_r, dist_r, dist_s,
+    loc_sem, a2a_s, kv_r, late_r, q_r, w_sem, fwd_s, x_s, x_r, c_s, c_r, y_sem, sq_s, sq_r, dist_r, dist_s,
 ):
     cores, HL, rows, DH = sizes
     width = HL * DH
@@ -204,17 +204,20 @@
 
     def spread(array, view, landing, recv_sems, both=False):
         for dx, dz in SPREAD:
-            send(view(head_at(dx, dz)), landing.at[own_slot], a2a_s.at[array], recv_sems.at[own_slot],
+            send(view(head_at(dx, dz)), landing.at[own_slot], a2a_s.at[array], recv_sems(own_slot),
                  {"heads": core if both and dz else 1 - core, "tokens": owner(dx, dz)})
 
+    def landed(array):
+        return lambda i: kv_r.at[array, i] if array < 2 else late_r.at[array - 2]
+
     def spread_keys(b):
-        spread(2 * b, lambda j: (k_hbm.at[b, :, cols(j)] if b else keys0.at[:, cols(j)]), kv.at[2 * b], kv_r.at[2 * b])
+        spread(2 * b, lambda j: (k_hbm.at[b, :, cols(j)] if b else keys0.at[:, cols(j)]), kv.at[2 * b], landed(2 * b))
 
     def spread_values(b):
-        spread(2 * b + 1, lambda j: dps.at[b, j], kv.at[2 * b + 1], kv_r.at[2 * b + 1])
+        spread(2 * b + 1, lambda j: dps.at[b, j], kv.at[2 * b + 1], landed(2 * b + 1))
 
     def spread_queries():
-        spread(4, lambda j: q_hbm.at[1, :, cols(j)], qb, q_r, both=True)
+        spread(4, lambda j: q_hbm.at[1, :, cols(j)], qb, lambda i: q_r.at[0], both=True)
 
     def scale_values(b):
         for j in range(HL):
@@ -239,7 +242,6 @@
     spread_values(0)
     local_v[1].wait()
     scale_values(1)
-    issue(0)
 
     def share_squares(b, square):
         sq[b] = jnp.broadcast_to(square, (rows, 128))
@@ -291,26 +293,23 @@
             dgu[i, :, half:] = (back * gate * sig).astype(BF16)
 
         if b == 0:
-            for k in WAITS:
+            for n, k in enumerate(WAITS):
                 i = slot(k)
                 arrived(kv.at[0, i], kv_r.at[0, i])
                 forward(0, i, away)
                 act[k] = mm(kv[0, i], weights)
+                issue(10 + n)
             for n, k in enumerate(WAITS):
                 i = slot(k)
                 arrived(kv.at[1, i], kv_r.at[1, i])
                 forward(1, i, away)
                 activations(i, act[k], mm_nt(kv[1, i], w_down))
-                if n == 3:
-                    issue(1)
-            issue(2)
+                issue(20 + n)
         else:
             @pl.when(home)
             def _():
-                for k in range(8):
-                    i = slot(k)
-                    arrived(kv.at[2, i], kv_r.at[2, i])
-                    arrived(kv.at[3, i], kv_r.at[3, i])
+                arrived(kv.at[2], late_r.at[0])
+                arrived(kv.at[3], late_r.at[1])
 
             for i in range(8):
                 activations(i, mm(kv[2, i], weights), mm_nt(kv[3, i], w_down))
@@ -357,20 +356,17 @@
 
     halve_weights(w_own)
     gradients(0, w_own)
-    issue(3)
     local_gain.wait()
     finish_block(0, lambda h: y0[:, h * DH:(h + 1) * DH])
-    for m in ORDER:
+    for n, m in enumerate(ORDER):
         exchange(0, m)
-    issue(4)
+        issue(30 + n)
 
     def pass_on(array):
         @pl.when(away)
         def _():
-            for k in range(8):
-                i = slot(k)
-                arrived(kv.at[array, i], kv_r.at[array, i])
-                send(kv.at[array, i], kv.at[array, i], fwd_s.at[array], kv_r.at[array, i], twin)
+            arrived(kv.at[array], late_r.at[array - 2])
+            send(kv.at[array], kv.at[array], fwd_s.at[array], late_r.at[array - 2], twin)
 
     if PASS_EARLY >= 1:
         pass_on(2)
@@ -390,8 +386,8 @@
         return (own_slot + 4 * home.astype(jnp.int32)) // 4 % 2 * 4 + k
 
     def new_outputs(first, last):
-        for k in range(first, last):
-            arrived(qb.at[slot_of(k)], q_r.at[slot_of(k)])
+        if first < last:
+            arrived(qb.at[pl.ds(0, 4)], q_r.at[0])
         for k in range(first, last):
             i = slot_of(k)
             ysend[k] = fast_net(qb[i], w1[GATE], w1[UP], w1[DOWN]).astype(BF16)
@@ -511,7 +507,7 @@
 
 WAITS = (0, 7, 3, 5, 6, 1, 2, 4)
 SPREAD = ((1, 1), (1, 0), (0, 1), (0, 0))
-ISSUE = (0, 1, 4)
+ISSUE = (11, 23, 32)
 PASS_EARLY = 2
 CUTS = (0, 4, 4, 4)
 
@@ -557,7 +553,7 @@
             vm((2, rows, 128), F32),
             vm((2, rows, 128), F32),
             dma(7),
-            dma(5), dma(4, 8), dma(8), dma(1), dma(6),
+            dma(5), dma(2, 8), dma(2), dma(1), dma(1), dma(6),
             dma(2), dma(2, 3), dma(2), dma(2, 3),
             dma(2), dma(2), dma(2),
             dma(4, 3, 2), dma(1),

time: 53.1 us -> 53.2 us (level)
  no operation moved by 1% of the time
where the time goes in v4:
time: 53.2 us; the launch traced here: 53.1 us
  Pallas kernels  52.4 us (98%)
  between operations  0.64 us (1%)
    pallas_call x1, Pallas kernels, one_kernel(): pl.pallas_call(functools.partial(kernel, (cores, HL, rows, DH)), out_shap...  51.1 us
    pallas_call x1, Pallas kernels, store(): pl.pallas_call(store_kernel, out_shape=(jax.ShapeDtypeStruct(mixed.shape,...  1.36 us

profile of v4, /device:TPU:0, one launch (start us, length us, event | category | flops | bytes accessed | tf_op | source)
XLA Modules:
  0.0 53.1 jit_solution(8297028595773087187)
XLA Ops:
  0.6 51.1 %shard_map.77 = (bf16[2,128,1024]{2,1,0:T(8,128)(2,1)S(1)}, bf16[4,3,256,256]{3,2,1,0:T(8,128)(2,1)S(1)}) custom-call(bf16[2,128,1024]{2,1,0:T(8,128)(2,1)} %q_hbm.1, bf16[2,128,1024]{2,1,0:T(8,128)(2,1)} %k_hbm.1, bf16[2,128,1024]{2,1,0:T(8,128)(2,1)} %v_hbm.1, f32[2,4,128]{2,1,0:T(4,128)} %r_hbm.1, bf16[4,3,256,256]{3,2,1,0:T(8,128)(2,1)} %w_hbm.1, ...), custom_call_target="tpu_custom_call" | custom-call | tf_op jit(solution)/shard_map/pallas_call | solution.py:523
  51.7 1.4 %shard_map.78 = (bf16[2,128,1024]{2,1,0:T(8,128)(2,1)}, bf16[4,3,256,256]{3,2,1,0:T(8,128)(2,1)}) custom-call(bf16[2,128,1024]{2,1,0:T(8,128)(2,1)S(1)} %get-tuple-element.4.mixed, bf16[4,3,256,256]{3,2,1,0:T(8,128)(2,1)S(1)} %get-tuple-element.5.weights), custom_call_target="tpu_custom_call" | custom-call | tf_op jit(solution)/shard_map/pallas_call | solution.py:576

commit v5 on v4

--- a/solution.py
+++ b/solution.py
@@ -506,8 +506,8 @@
 
 
 WAITS = (0, 7, 3, 5, 6, 1, 2, 4)
-SPREAD = ((1, 1), (1, 0), (0, 1), (0, 0))
-ISSUE = (11, 23, 32)
+SPREAD = ((1, 1), (0, 1), (1, 0), (0, 0))
+ISSUE = (10, 23, 32)
 PASS_EARLY = 2
 CUTS = (0, 4, 4, 4)
 

time: 53.2 us -> 52.9 us (level)
  no operation moved by 1% of the time
where the time goes in v5:
time: 52.9 us; the launch traced here: 52.8 us
  Pallas kernels  52.1 us (98%)
  between operations  0.64 us (1%)
    pallas_call x1, Pallas kernels, one_kernel(): pl.pallas_call(functools.partial(kernel, (cores, HL, rows, DH)), out_shap...  50.8 us
    pallas_call x1, Pallas kernels, store(): pl.pallas_call(store_kernel, out_shape=(jax.ShapeDtypeStruct(mixed.shape,...  1.36 us

profile of v5, /device:TPU:0, one launch (start us, length us, event | category | flops | bytes accessed | tf_op | source)
XLA Modules:
  0.0 52.8 jit_solution(6504619199220839077)
XLA Ops:
  0.6 50.8 %shard_map.77 = (bf16[2,128,1024]{2,1,0:T(8,128)(2,1)S(1)}, bf16[4,3,256,256]{3,2,1,0:T(8,128)(2,1)S(1)}) custom-call(bf16[2,128,1024]{2,1,0:T(8,128)(2,1)} %q_hbm.1, bf16[2,128,1024]{2,1,0:T(8,128)(2,1)} %k_hbm.1, bf16[2,128,1024]{2,1,0:T(8,128)(2,1)} %v_hbm.1, f32[2,4,128]{2,1,0:T(4,128)} %r_hbm.1, bf16[4,3,256,256]{3,2,1,0:T(8,128)(2,1)} %w_hbm.1, ...), custom_call_target="tpu_custom_call" | custom-call | tf_op jit(solution)/shard_map/pallas_call | solution.py:523
  51.4 1.4 %shard_map.78 = (bf16[2,128,1024]{2,1,0:T(8,128)(2,1)}, bf16[4,3,256,256]{3,2,1,0:T(8,128)(2,1)}) custom-call(bf16[2,128,1024]{2,1,0:T(8,128)(2,1)S(1)} %get-tuple-element.4.mixed, bf16[4,3,256,256]{3,2,1,0:T(8,128)(2,1)S(1)} %get-tuple-element.5.weights), custom_call_target="tpu_custom_call" | custom-call | tf_op jit(solution)/shard_map/pallas_call | solution.py:576

commit v6 on v5

--- a/solution.py
+++ b/solution.py
@@ -108,7 +108,7 @@
     for g in mats:
         g = g.astype(F32)
         square = jnp.sum(jnp.sum(g * g, axis=1, keepdims=True), axis=0, keepdims=True)
-        xs.append((g / (jnp.sqrt(square) + 1e-07)).astype(BF16))
+        xs.append((g * (1.0 / (jnp.sqrt(square) + 1e-07))).astype(BF16))
     for _ in range(NS_STEPS):
         grams = [mm_nt(x, x).astype(BF16) for x in xs]
         mixers = [(coef_b * a.astype(F32) + coef_c * mm(a, a)).astype(BF16) for a in grams]
@@ -180,6 +180,17 @@
     local_k.start()
     local_r.start()
     local_v[0].start()
+    barrier = pltpu.get_barrier_semaphore()
+
+    @pl.when(away)
+    def _():
+        for k in range(8):
+            pl.semaphore_signal(
+                barrier, inc=1, device_id={"heads": 1 - core, "tokens": slot(k) + 8 * zh}, device_id_type=MESH
+            )
+
+    for device in ({"heads": 1 - core}, *({"tokens": chip} for chip in (mate, x_near, y_near, z_near))):
+        pl.semaphore_signal(barrier, inc=1, device_id=device, device_id_type=MESH)
     local_w.start()
     local_q.start()
     local_v[1].start()
@@ -189,17 +200,6 @@
     def _():
         own_w.start()
 
-    barrier = pltpu.get_barrier_semaphore()
-
-    @pl.when(away)
-    def _():
-        for k in range(8):
-            pl.semaphore_signal(
-                barrier, inc=1, device_id={"heads": 1 - core, "tokens": slot(k) + 8 * zh}, device_id_type=MESH
-            )
-
-    for device in ({"heads": 1 - core}, *({"tokens": chip} for chip in (mate, x_near, y_near, z_near))):
-        pl.semaphore_signal(barrier, inc=1, device_id=device, device_id_type=MESH)
     pl.semaphore_wait(barrier, HL + 5)
 
     def spread(array, view, landing, recv_sems, both=False):

time: 52.9 us -> 52.9 us (level)
  no operation moved by 1% of the time
where the time goes in v6:
time: 52.9 us; the launch traced here: 52.8 us
  Pallas kernels  52.1 us (98%)
  between operations  0.64 us (1%)
    pallas_call x1, Pallas kernels, one_kernel(): pl.pallas_call(functools.partial(kernel, (cores, HL, rows, DH)), out_shap...  50.8 us
    pallas_call x1, Pallas kernels, store(): pl.pallas_call(store_kernel, out_shape=(jax.ShapeDtypeStruct(mixed.shape,...  1.36 us

profile of v6, /device:TPU:0, one launch (start us, length us, event | category | flops | bytes accessed | tf_op | source)
XLA Modules:
  0.0 52.8 jit_solution(12848411977221645334)
XLA Ops:
  0.6 50.8 %shard_map.77 = (bf16[2,128,1024]{2,1,0:T(8,128)(2,1)S(1)}, bf16[4,3,256,256]{3,2,1,0:T(8,128)(2,1)S(1)}) custom-call(bf16[2,128,1024]{2,1,0:T(8,128)(2,1)} %q_hbm.1, bf16[2,128,1024]{2,1,0:T(8,128)(2,1)} %k_hbm.1, bf16[2,128,1024]{2,1,0:T(8,128)(2,1)} %v_hbm.1, f32[2,4,128]{2,1,0:T(4,128)} %r_hbm.1, bf16[4,3,256,256]{3,2,1,0:T(8,128)(2,1)} %w_hbm.1, ...), custom_call_target="tpu_custom_call" | custom-call | tf_op jit(solution)/shard_map/pallas_call | solution.py:523
  51.4 1.4 %shard_map.78 = (bf16[2,128,1024]{2,1,0:T(8,128)(2,1)}, bf16[4,3,256,256]{3,2,1,0:T(8,128)(2,1)}) custom-call(bf16[2,128,1024]{2,1,0:T(8,128)(2,1)S(1)} %get-tuple-element.4.mixed, bf16[4,3,256,256]{3,2,1,0:T(8,128)(2,1)S(1)} %get-tuple-element.5.weights), custom_call_target="tpu_custom_call" | custom-call | tf_op jit(solution)/shard_map/pallas_call | solution.py:576
